TPU v7x, 256 devices: a whole 4x4x8 slice. The times are simulated.
256 devices in a mesh: sub: 4 (over z_lo), coarse: 64 (over x, z_hi, y, core).
Axes of the slice: x: 4, y: 4, z: 8 (z_hi: 2, z_lo: 4; z = z_hi * 4 + z_lo), core: 2. Of those that a mesh axis runs over, the one named last changes fastest.
Arguments:
- schur_inverse: bfloat16 [512, 1536, 1536], P(('sub', 'coarse')), may hold values from -1 to 2, as said below
- corner_coupling: bfloat16 [512, 24, 1536], P(('sub', 'coarse')), may hold values from -0.21875 to 0.21875
- coarse_inverse: bfloat16 [4, 64, 24, 6144], P(None, 'coarse', None, 'sub'), may hold values from -1 to 2
- load_cases: bfloat16 [512, 16, 1536], P(('sub', 'coarse')), may hold values from -16 to 16
- face_order: int32 [512, 768], P(('sub', 'coarse')), may hold values from 0 to 767, each once within a row
- corner_dofs: int32 [512, 24], P(('sub', 'coarse')), may hold values from 0 to 6143, as said below
- scene_loads: int32 [128, 2], replicated, may hold values from 0 to 15
- scene_weights: float32 [128, 2], replicated, may hold values from 0.3 to 3
Outputs:
- multipliers: float32 [512, 128, 768], P(('sub', 'coarse'))
- residual: float32 [512, 128, 768], P(('sub', 'coarse'))
Inputs may be any that keep to these rules, and one draw needn't show every extreme that they name: `schur_inverse`: each subdomain's block is symmetric positive definite. `corner_dofs`: every entry of row n has the form (a * 64 + c) * 24 + r with c the group of subdomain n, 0 <= a < 4 and 0 <= r < 24; every coarse dof of a group is named by exactly 2 entries of that group's rows.
All inputs are finite; a program needn't handle non-finite values.
Results may differ from a plain program's by a relative error of at most 0.034.
Values may be sent and summed in bfloat16 or wider, within the bound.
A program may use at most 64 MiB of HBM per device.

v0:
```python
import functools

import jax
import jax.numpy as jnp
from jax import lax
from jax.sharding import Mesh
from jax.sharding import PartitionSpec as P

ITERS = 2
SUB_COARSE = ("sub", "coarse_0", "coarse_1", "coarse_2", "coarse_3")
COARSE = ("coarse_0", "coarse_1", "coarse_2", "coarse_3")


def by_axis(array, axes):
    return functools.reduce(lax.psum, axes, array)


def shifted(array, axis, by):
    length = lax.axis_size(axis)
    pairs = [(i, i + by) for i in range(length) if 0 <= i + by < length]
    return lax.ppermute(array, axis, pairs)


def in_blocks(array, dim, length):
    dims = array.shape
    blocks = array.reshape(*dims[:dim], length, dims[dim] // length, *dims[dim + 1 :])
    return jnp.moveaxis(blocks, dim, 0)


def sent_and_summed(array, axis, dim):
    blocks = in_blocks(array, dim, lax.axis_size(axis))
    arrived = lax.all_to_all(blocks, axis, split_axis=0, concat_axis=0, tiled=True)
    return arrived.sum(axis=0)


def in_order(blocks, dim):
    dims = list(blocks.shape[1:])
    dims[dim] *= blocks.shape[0]
    return jnp.moveaxis(blocks, 0, dim).reshape(dims)


def from_everyone(array, axis):
    copies = jnp.broadcast_to(array, (lax.axis_size(axis), *array.shape))
    return lax.all_to_all(copies, axis, split_axis=0, concat_axis=0, tiled=True)


def gather_directly(array, axis, dim):
    return in_order(from_everyone(array, axis), dim)


def over_copies(array, axis):
    return from_everyone(array, axis).astype(jnp.float32).sum(axis=0)


def three_sums(local_values):
    return (
        by_axis(local_values[0], SUB_COARSE),
        by_axis(local_values[1], SUB_COARSE),
        by_axis(local_values[2], SUB_COARSE),
    )


def per_device(
    schur_inverse,
    corner_coupling,
    coarse_inverse,
    load_cases,
    face_order,
    corner_dofs,
    scene_loads,
    scene_weights,
):
    local_subs = schur_inverse.shape[0]
    face_size = face_order.shape[1]
    corner_count = corner_dofs.shape[1]
    scene_count = scene_weights.shape[0]
    coarse_devices = lax.axis_size(COARSE)
    column_size = lax.axis_size("sub") * corner_count
    face_ids = jnp.arange(face_size, dtype=jnp.int32)
    forward_table = (face_order[:, None, :] == face_ids[None, :, None]).astype(jnp.float32)
    backward_table = (face_order[:, :, None] == face_ids[None, None, :]).astype(jnp.bfloat16)
    local_index = (
        corner_dofs // (coarse_devices * corner_count) * corner_count + corner_dofs % corner_count
    )
    flat_index = local_index.reshape(-1)
    column_ids = jnp.arange(column_size, dtype=jnp.int32)
    assemble = (column_ids[:, None] == flat_index[None, :]).astype(jnp.float32)
    spread = (flat_index[:, None] == column_ids[None, :]).astype(jnp.bfloat16)
    kernel_rows = coarse_inverse.reshape(column_size, coarse_inverse.shape[3])
    head_mask = jnp.logical_and(jnp.arange(local_subs) == 0, lax.axis_index("sub") == 0)[
        :, None, None
    ]

    def jump(displaced):
        outgoing = displaced[local_subs - 1, :, face_size:]
        incoming = shifted(outgoing.astype(jnp.bfloat16), "sub", 1).astype(outgoing.dtype)
        previous = jnp.concatenate([incoming[None], displaced[:-1, :, face_size:]], axis=0)
        permuted = lax.dot_general(
            previous,
            forward_table,
            (((2,), (1,)), ((0,), (0,))),
            preferred_element_type=jnp.float32,
        )
        return jnp.where(head_mask, 0.0, permuted - displaced[:, :, :face_size])

    def primal_solve(loads):
        corner_terms = lax.dot_general(
            corner_coupling, loads, (((2,), (2,)), ((0,), (0,))), preferred_element_type=jnp.float32
        )
        column_terms = jnp.dot(
            assemble, corner_terms.reshape(-1, scene_count), preferred_element_type=jnp.float32
        )
        owned_piece = sent_and_summed(column_terms, "sub", 0).astype(jnp.bfloat16)
        partial_value = jnp.dot(
            kernel_rows, gather_directly(owned_piece, COARSE, 0), preferred_element_type=jnp.float32
        )
        coarse_values = (
            over_copies(partial_value.astype(jnp.bfloat16), "sub")
            .astype(jnp.float32)
            .astype(jnp.bfloat16)
        )
        corner_values = jnp.dot(spread, coarse_values, preferred_element_type=jnp.float32).astype(
            jnp.bfloat16
        )
        corner_values = corner_values.reshape(local_subs, corner_count, scene_count)
        local_part = lax.dot_general(
            loads, schur_inverse, (((2,), (1,)), ((0,), (0,))), preferred_element_type=jnp.float32
        )
        coarse_part = lax.dot_general(
            corner_values,
            corner_coupling,
            (((1,), (1,)), ((0,), (0,))),
            preferred_element_type=jnp.float32,
        )
        return local_part + coarse_part

    selection = (
        scene_loads[:, :, None] == jnp.arange(load_cases.shape[1], dtype=jnp.int32)[None, None, :]
    ).astype(jnp.float32)
    mixing = jnp.sum(selection * scene_weights[:, :, None], axis=1)
    external = jnp.einsum("sl,nlb->nsb", mixing, load_cases.astype(jnp.float32)).astype(
        jnp.bfloat16
    )
    residual = jump(primal_solve(external))
    direction = residual
    multipliers = jnp.zeros_like(residual)
    start_local = jnp.sum(residual * residual, axis=(0, 2))
    norm_now = by_axis(start_local, SUB_COARSE)
    for iteration in range(ITERS):
        values = direction.astype(jnp.bfloat16)
        moved = lax.dot_general(
            values, backward_table, (((2,), (1,)), ((0,), (0,))), preferred_element_type=jnp.float32
        ).astype(jnp.bfloat16)
        transposed_incoming = shifted(moved[0], "sub", -1)
        right_faces = jnp.concatenate([moved[1:], transposed_incoming[None]], axis=0)
        image_dir = jump(primal_solve(jnp.concatenate([-values, right_faces], axis=2)))
        local_values = (
            jnp.sum(direction * image_dir, axis=(0, 2)),
            jnp.sum(residual * image_dir, axis=(0, 2)),
            jnp.sum(image_dir * image_dir, axis=(0, 2)),
        )
        if iteration == 0:
            curvature, cross_term, image_norm = three_sums(local_values)
        else:
            curvature, cross_term, image_norm = three_sums(local_values)
        step_size = norm_now / curvature
        multipliers = multipliers + step_size[None, :, None] * direction
        residual = residual - step_size[None, :, None] * image_dir
        if iteration + 1 < ITERS:
            norm_next = norm_now - 2.0 * step_size * cross_term + step_size * step_size * image_norm
            direction = residual + (norm_next / norm_now)[None, :, None] * direction
            norm_now = norm_next
    return (multipliers, residual)


def solution(mesh):
    finer = Mesh(
        mesh.devices.reshape(mesh.shape["sub"], 4, 2, 4, 2),
        ("sub", "coarse_0", "coarse_1", "coarse_2", "coarse_3"),
    )
    return jax.shard_map(
        per_device,
        mesh=finer,
        in_specs=(
            P(SUB_COARSE, None, None),
            P(SUB_COARSE, None, None),
            P(None, COARSE, None, "sub"),
            P(SUB_COARSE, None, None),
            P(SUB_COARSE, None),
            P(SUB_COARSE, None),
            P(),
            P(),
        ),
        out_specs=(P(SUB_COARSE, None, None), P(SUB_COARSE, None, None)),
        check_vma=False,
    )
```

profile of v0, /device:TPU:1, one launch (start us, length us, event | category | flops | bytes accessed | tf_op | source)
XLA Modules:
  0.0 277.6 jit_solution(12648108814154664489)
XLA Ops:
  4.9 10.8 %all_to_all.45 = f32[4,24,128]{2,1,0:T(8,128)S(1)} all-to-all(f32[4,24,128]{2,1,0:T(8,128)S(1)} %fusion.42), channel_id=1, replica_groups=mesh['sub'=4,'coarse_0'=4,'coarse_1'=2,'coarse_2'=4,'coarse_3'=2] {'sub'}, dimensions={0} | all-to-all | bytes 98304 | tf_op jit(solution)/shard_map/all_to_all | solution.py:32
  15.7 30.3 %all_to_all.46 = bf16[64,24,128]{2,1,0:T(8,128)(2,1)S(1)} all-to-all(bf16[64,24,128]{2,1,0:T(8,128)(2,1)S(1)} %broadcast_in_dim.79), channel_id=1, replica_groups=mesh['sub'=4,'coarse_0'=4,'coarse_1'=2,'coarse_2'=4,'coarse_3'=2] {'coar..., dimensions={0} | all-to-all | bytes 786432 | tf_op jit(solution)/shard_map/all_to_all | solution.py:44
  46.9 4.1 %all-to-all-start.2 = ((bf16[4,96,128]{2,1,0:T(8,128)(2,1)}), bf16[4,96,128]{2,1,0:T(8,128)(2,1)S(1)}, u32[]{:S(2)}, u32[]{:S(2)}) async-start(bf16[4,96,128]{2,1,0:T(8,128)(2,1)} %broadcast_in_dim.80), calls=%async_computation.2 | async-start | bytes 196608 | tf_op jit(solution)/shard_map/all_to_all | solution.py:44
  51.1 5.1 %fusion.65 = f32[2,128,1536]{2,1,0:T(8,128)S(1)} fusion(bf16[2,128,1536]{2,1,0:T(8,128)(2,1)S(1)} %fusion.5, bf16[2,1536,1536]{2,1,0:T(8,128)(2,1)} %param.8), kind=kOutput, calls=%fused_computation.105 | convolution fusion | flops 1207959552 | bytes 11796480 | tf_op jit(solution)/shard_map/dot_general | solution.py:126
  58.0 4.0 %collective-permute-start = (bf16[128,768]{1,0:T(8,128)(2,1)S(1)}, bf16[128,768]{1,0:T(8,128)(2,1)S(1)}, u32[]{:S(2)}, u32[]{:S(2)}) collective-permute-start(bf16[128,768]{1,0:T(8,128)(2,1)S(1)} %get-tuple-element.29), channel_id=1, source_target_pairs={{0,64},{64,128},{128,192},{1,65},{65,129},{129,193},{2,66},{66,130... | collective-permute-start | bytes 589832 | tf_op jit(solution)/shard_map/ppermute | solution.py:21
  62.0 3.7 %collective-permute-done = bf16[128,768]{1,0:T(8,128)(2,1)S(1)} collective-permute-done((bf16[128,768]{1,0:T(8,128)(2,1)S(1)}, bf16[128,768]{1,0:T(8,128)(2,1)S(1)}, u32[]{:S(2)}, u32[]{:S(2)}) %collective-permute-start) | collective-permute-done | bytes 196640 | tf_op jit(solution)/shard_map/ppermute | solution.py:21
  65.7 2.2 convert_negate_fusion.1
  70.4 6.7 %collective-permute-done.1 = bf16[128,768]{1,0:T(8,128)(2,1)S(1)} collective-permute-done((bf16[128,768]{1,0:T(8,128)(2,1)S(1)}, bf16[128,768]{1,0:T(8,128)(2,1)S(1)}, u32[]{:S(2)}, u32[]{:S(2)}) %collective-permute-start.1) | collective-permute-done | bytes 196640 | tf_op jit(solution)/shard_map/ppermute | solution.py:21
  77.6 6.9 %all_to_all.47 = f32[4,24,128]{2,1,0:T(8,128)S(1)} all-to-all(f32[4,24,128]{2,1,0:T(8,128)S(1)} %fusion.40), channel_id=1, replica_groups=mesh['sub'=4,'coarse_0'=4,'coarse_1'=2,'coarse_2'=4,'coarse_3'=2] {'sub'}, dimensions={0} | all-to-all | bytes 98304 | tf_op jit(solution)/shard_map/all_to_all | solution.py:32
  84.6 23.9 %all_to_all.48 = bf16[64,24,128]{2,1,0:T(8,128)(2,1)S(1)} all-to-all(bf16[64,24,128]{2,1,0:T(8,128)(2,1)S(1)} %broadcast_in_dim.84), channel_id=1, replica_groups=mesh['sub'=4,'coarse_0'=4,'coarse_1'=2,'coarse_2'=4,'coarse_3'=2] {'coar..., dimensions={0} | all-to-all | bytes 786432 | tf_op jit(solution)/shard_map/all_to_all | solution.py:44
  108.8 8.6 %all_to_all.49 = bf16[4,96,128]{2,1,0:T(8,128)(2,1)S(1)} all-to-all(bf16[4,96,128]{2,1,0:T(8,128)(2,1)S(1)} %broadcast_in_dim.85), channel_id=1, replica_groups=mesh['sub'=4,'coarse_0'=4,'coarse_1'=2,'coarse_2'=4,'coarse_3'=2] {'sub'}, dimensions={0} | all-to-all | bytes 196608 | tf_op jit(solution)/shard_map/all_to_all | solution.py:44
  118.0 5.1 %convolution_add_fusion.2 = f32[2,128,1536]{2,1,0:T(8,128)S(1)} fusion(f32[2,128,1536]{2,1,0:T(8,128)S(1)} %fusion.67, bf16[2,1536,1536]{2,1,0:T(8,128)(2,1)} %param.8, bf16[1,128,768]{2,1,0:T(8,128)(2,1)S(1)} %bitcast.93, bf16[1,128,768]{2,1,0:T(8,128)(2,1)S(1)} %get-tuple-element.35, bf16[2,128,768]{2,1,0:T(8,128)(2,1)S(1)} %get-tuple-element.37), kind=kOutput, calls=%fused_computation.9 | convolution fusion | flops 1210712064 | bytes 13369344 | tf_op jit(solution)/shard_map/dot_general | solution.py:126
  123.1 2.8 %collective-permute-start.2 = (bf16[128,768]{1,0:T(8,128)(2,1)S(1)}, bf16[128,768]{1,0:T(8,128)(2,1)S(1)}, u32[]{:S(2)}, u32[]{:S(2)}) collective-permute-start(bf16[128,768]{1,0:T(8,128)(2,1)S(1)} %get-tuple-element.27), channel_id=1, source_target_pairs={{0,64},{64,128},{128,192},{1,65},{65,129},{129,193},{2,66},{66,130... | collective-permute-start | bytes 589832 | tf_op jit(solution)/shard_map/ppermute | solution.py:21
  126.0 2.6 collective-permute-done.2
  129.8 10.1 %all-reduce.2 = (f32[128]{0:T(128)S(1)}, f32[128]{0:T(128)S(1)}, f32[128]{0:T(128)S(1)}) all-reduce(f32[128]{0:T(128)S(1)} %get-tuple-element.3, f32[128]{0:T(128)S(1)} %get-tuple-element.4, f32[128]{0:T(128)S(1)} %get-tuple-element.2), channel_id=1, replica_groups=mesh['sub'=4,'coarse_0'=4,'coarse_1'=2,'coarse_2'=4,'coarse_3'=2] {'sub'}, use_global_device_ids=true, to_apply=%region_18.19 | all-reduce | flops 384 | bytes 3072 | tf_op jit(solution)/shard_map/psum | solution.py:15
  139.9 6.8 %all-reduce.1 = (f32[128]{0:T(128)S(1)}, f32[128]{0:T(128)S(1)}, f32[128]{0:T(128)S(1)}) all-reduce(f32[128]{0:T(128)S(1)} %get-tuple-element.11, f32[128]{0:T(128)S(1)} %get-tuple-element.12, f32[128]{0:T(128)S(1)} %get-tuple-element.13), channel_id=1, replica_groups=mesh['sub'=4,'coarse_0'=4,'coarse_1'=2,'coarse_2'=4,'coarse_3'=2] {'coar..., use_global_device_ids=true, to_apply=%region_19.20 | all-reduce | flops 384 | bytes 3072 | tf_op jit(solution)/shard_map/psum | solution.py:15
  146.7 7.7 %all-reduce.4 = (f32[128]{0:T(128)S(1)}, f32[128]{0:T(128)S(1)}, f32[128]{0:T(128)S(1)}) all-reduce(f32[128]{0:T(128)S(1)} %get-tuple-element.8, f32[128]{0:T(128)S(1)} %get-tuple-element.9, f32[128]{0:T(128)S(1)} %get-tuple-element.10), channel_id=1, replica_groups=mesh['sub'=4,'coarse_0'=4,'coarse_1'=2,'coarse_2'=4,'coarse_3'=2] {'coar..., use_global_device_ids=true, to_apply=%region_20.21 | all-reduce | flops 384 | bytes 3072 | tf_op jit(solution)/shard_map/psum | solution.py:15
  154.4 6.8 %all-reduce = (f32[128]{0:T(128)S(1)}, f32[128]{0:T(128)S(1)}, f32[128]{0:T(128)S(1)}) all-reduce(f32[128]{0:T(128)S(1)} %get-tuple-element.17, f32[128]{0:T(128)S(1)} %get-tuple-element.18, f32[128]{0:T(128)S(1)} %get-tuple-element.19), channel_id=1, replica_groups=mesh['sub'=4,'coarse_0'=4,'coarse_1'=2,'coarse_2'=4,'coarse_3'=2] {'coar..., use_global_device_ids=true, to_apply=%region_21.22 | all-reduce | flops 384 | bytes 3072 | tf_op jit(solution)/shard_map/psum | solution.py:15
  161.2 11.1 %all-reduce.3 = (f32[128]{0:T(128)S(1)}, f32[128]{0:T(128)S(1)}, f32[128]{0:T(128)S(1)}) all-reduce(f32[128]{0:T(128)S(1)} %get-tuple-element.5, f32[128]{0:T(128)S(1)} %get-tuple-element.6, f32[128]{0:T(128)S(1)} %get-tuple-element.7), channel_id=1, replica_groups=mesh['sub'=4,'coarse_0'=4,'coarse_1'=2,'coarse_2'=4,'coarse_3'=2] {'coar..., use_global_device_ids=true, to_apply=%region_22.23 | all-reduce | flops 384 | bytes 3072 | tf_op jit(solution)/shard_map/psum | solution.py:15
  173.7 1.5 collective-permute-start.3
  175.2 6.5 %collective-permute-done.3 = bf16[128,768]{1,0:T(8,128)(2,1)S(1)} collective-permute-done((bf16[128,768]{1,0:T(8,128)(2,1)S(1)}, bf16[128,768]{1,0:T(8,128)(2,1)S(1)}, u32[]{:S(2)}, u32[]{:S(2)}) %collective-permute-start.3) | collective-permute-done | bytes 196640 | tf_op jit(solution)/shard_map/ppermute | solution.py:21
  182.6 6.9 %all_to_all.50 = f32[4,24,128]{2,1,0:T(8,128)S(1)} all-to-all(f32[4,24,128]{2,1,0:T(8,128)S(1)} %fusion.38), channel_id=1, replica_groups=mesh['sub'=4,'coarse_0'=4,'coarse_1'=2,'coarse_2'=4,'coarse_3'=2] {'sub'}, dimensions={0} | all-to-all | bytes 98304 | tf_op jit(solution)/shard_map/all_to_all | solution.py:32
  189.5 22.7 %all_to_all.51 = bf16[64,24,128]{2,1,0:T(8,128)(2,1)S(1)} all-to-all(bf16[64,24,128]{2,1,0:T(8,128)(2,1)S(1)} %broadcast_in_dim.89), channel_id=1, replica_groups=mesh['sub'=4,'coarse_0'=4,'coarse_1'=2,'coarse_2'=4,'coarse_3'=2] {'coar..., dimensions={0} | all-to-all | bytes 786432 | tf_op jit(solution)/shard_map/all_to_all | solution.py:44
  212.5 8.6 %all_to_all.52 = bf16[4,96,128]{2,1,0:T(8,128)(2,1)S(1)} all-to-all(bf16[4,96,128]{2,1,0:T(8,128)(2,1)S(1)} %broadcast_in_dim.90), channel_id=1, replica_groups=mesh['sub'=4,'coarse_0'=4,'coarse_1'=2,'coarse_2'=4,'coarse_3'=2] {'sub'}, dimensions={0} | all-to-all | bytes 196608 | tf_op jit(solution)/shard_map/all_to_all | solution.py:44
  222.1 5.1 %convolution_add_fusion.1 = f32[2,128,1536]{2,1,0:T(8,128)S(1)} fusion(f32[2,128,1536]{2,1,0:T(8,128)S(1)} %fusion.68, bf16[2,1536,1536]{2,1,0:T(8,128)(2,1)} %param.8, bf16[1,128,768]{2,1,0:T(8,128)(2,1)S(1)} %bitcast.91, bf16[1,128,768]{2,1,0:T(8,128)(2,1)S(1)} %get-tuple-element.33, bf16[2,128,768]{2,1,0:T(8,128)(2,1)S(1)} %get-tuple-element.20), kind=kOutput, calls=%fused_computation.8 | convolution fusion | flops 1210712064 | bytes 13369344 | tf_op jit(solution)/shard_map/dot_general | solution.py:126
  227.2 2.8 %collective-permute-start.4 = (bf16[128,768]{1,0:T(8,128)(2,1)S(1)}, bf16[128,768]{1,0:T(8,128)(2,1)S(1)}, u32[]{:S(2)}, u32[]{:S(2)}) collective-permute-start(bf16[128,768]{1,0:T(8,128)(2,1)S(1)} %get-tuple-element.25), channel_id=1, source_target_pairs={{0,64},{64,128},{128,192},{1,65},{65,129},{129,193},{2,66},{66,130... | collective-permute-start | bytes 589832 | tf_op jit(solution)/shard_map/ppermute | solution.py:21
  230.0 2.6 collective-permute-done.4
  233.8 10.1 %psum.170 = f32[128]{0:T(128)S(1)} all-reduce(f32[128]{0:T(128)S(1)} %get-tuple-element.40), channel_id=1, replica_groups=mesh['sub'=4,'coarse_0'=4,'coarse_1'=2,'coarse_2'=4,'coarse_3'=2] {'sub'}, use_global_device_ids=true, to_apply=%region_26.27 | all-reduce | flops 128 | bytes 1024 | tf_op jit(solution)/shard_map/psum | solution.py:15
  243.8 6.8 %psum.171 = f32[128]{0:T(128)S(1)} all-reduce(f32[128]{0:T(128)S(1)} %psum.170), channel_id=1, replica_groups=mesh['sub'=4,'coarse_0'=4,'coarse_1'=2,'coarse_2'=4,'coarse_3'=2] {'coar..., use_global_device_ids=true, to_apply=%region_27.28 | all-reduce | flops 128 | bytes 1024 | tf_op jit(solution)/shard_map/psum | solution.py:15
  250.6 7.7 %psum.172 = f32[128]{0:T(128)S(1)} all-reduce(f32[128]{0:T(128)S(1)} %psum.171), channel_id=1, replica_groups=mesh['sub'=4,'coarse_0'=4,'coarse_1'=2,'coarse_2'=4,'coarse_3'=2] {'coar..., use_global_device_ids=true, to_apply=%region_28.29 | all-reduce | flops 128 | bytes 1024 | tf_op jit(solution)/shard_map/psum | solution.py:15
  258.3 6.8 %psum.173 = f32[128]{0:T(128)S(1)} all-reduce(f32[128]{0:T(128)S(1)} %psum.172), channel_id=1, replica_groups=mesh['sub'=4,'coarse_0'=4,'coarse_1'=2,'coarse_2'=4,'coarse_3'=2] {'coar..., use_global_device_ids=true, to_apply=%region_29.30 | all-reduce | flops 128 | bytes 1024 | tf_op jit(solution)/shard_map/psum | solution.py:15
  265.1 11.1 %psum.174 = f32[128]{0:T(128)S(1)} all-reduce(f32[128]{0:T(128)S(1)} %psum.173), channel_id=1, replica_groups=mesh['sub'=4,'coarse_0'=4,'coarse_1'=2,'coarse_2'=4,'coarse_3'=2] {'coar..., use_global_device_ids=true, to_apply=%region_30.31 | all-reduce | flops 128 | bytes 1024 | tf_op jit(solution)/shard_map/psum | solution.py:15
  (60 shorter events, 18.3 us)
Async XLA Ops:
  0.6 45.4 %copy-start = (bf16[4,1,24,1536]{3,2,1,0:T(8,128)(2,1)S(1)}, bf16[4,1,24,1536]{3,2,1,0:T(8,128)(2,1)}, u32[]{:S(2)}) copy-start(bf16[4,1,24,1536]{3,2,1,0:T(8,128)(2,1)} %param.10) | copy-start | bytes 884740
  46.9 9.2 %all-to-all-start.2 = ((bf16[4,96,128]{2,1,0:T(8,128)(2,1)}), bf16[4,96,128]{2,1,0:T(8,128)(2,1)S(1)}, u32[]{:S(2)}, u32[]{:S(2)}) async-start(bf16[4,96,128]{2,1,0:T(8,128)(2,1)} %broadcast_in_dim.80), calls=%async_computation.2 | async-start | bytes 196608 | tf_op jit(solution)/shard_map/all_to_all | solution.py:44
  51.1 5.3 %copy-start.2 = (bf16[2,24,1536]{2,1,0:T(8,128)(2,1)S(1)}, bf16[2,24,1536]{2,1,0:T(8,128)(2,1)}, u32[]{:S(2)}) copy-start(bf16[2,24,1536]{2,1,0:T(8,128)(2,1)} %param.9) | copy-start | bytes 442372
  56.4 9.3 %copy-start.5 = (s32[2,768]{1,0:T(2,128)S(1)}, s32[2,768]{1,0:T(2,128)}, u32[]{:S(2)}) copy-start(s32[2,768]{1,0:T(2,128)} %param.12) | copy-start | bytes 18436
  56.8 1.2 copy-start.1
  58.0 7.7 %collective-permute-start = (bf16[128,768]{1,0:T(8,128)(2,1)S(1)}, bf16[128,768]{1,0:T(8,128)(2,1)S(1)}, u32[]{:S(2)}, u32[]{:S(2)}) collective-permute-start(bf16[128,768]{1,0:T(8,128)(2,1)S(1)} %get-tuple-element.29), channel_id=1, source_target_pairs={{0,64},{64,128},{128,192},{1,65},{65,129},{129,193},{2,66},{66,130... | collective-permute-start | bytes 589832 | tf_op jit(solution)/shard_map/ppermute | solution.py:21
  69.1 8.0 %collective-permute-start.1 = (bf16[128,768]{1,0:T(8,128)(2,1)S(1)}, bf16[128,768]{1,0:T(8,128)(2,1)S(1)}, u32[]{:S(2)}, u32[]{:S(2)}) collective-permute-start(bf16[128,768]{1,0:T(8,128)(2,1)S(1)} %get-tuple-element.36), channel_id=1, source_target_pairs={{64,0},{128,64},{192,128},{65,1},{129,65},{193,129},{66,2},{130,66... | collective-permute-start | bytes 589832 | tf_op jit(solution)/shard_map/ppermute | solution.py:21
  123.1 5.4 %collective-permute-start.2 = (bf16[128,768]{1,0:T(8,128)(2,1)S(1)}, bf16[128,768]{1,0:T(8,128)(2,1)S(1)}, u32[]{:S(2)}, u32[]{:S(2)}) collective-permute-start(bf16[128,768]{1,0:T(8,128)(2,1)S(1)} %get-tuple-element.27), channel_id=1, source_target_pairs={{0,64},{64,128},{128,192},{1,65},{65,129},{129,193},{2,66},{66,130... | collective-permute-start | bytes 589832 | tf_op jit(solution)/shard_map/ppermute | solution.py:21
  173.7 8.0 %collective-permute-start.3 = (bf16[128,768]{1,0:T(8,128)(2,1)S(1)}, bf16[128,768]{1,0:T(8,128)(2,1)S(1)}, u32[]{:S(2)}, u32[]{:S(2)}) collective-permute-start(bf16[128,768]{1,0:T(8,128)(2,1)S(1)} %get-tuple-element.34), channel_id=1, source_target_pairs={{64,0},{128,64},{192,128},{65,1},{129,65},{193,129},{66,2},{130,66... | collective-permute-start | bytes 589832 | tf_op jit(solution)/shard_map/ppermute | solution.py:21
  181.7 0.7 copy-start.3
  221.1 0.9 copy-start.4
  227.2 5.4 %collective-permute-start.4 = (bf16[128,768]{1,0:T(8,128)(2,1)S(1)}, bf16[128,768]{1,0:T(8,128)(2,1)S(1)}, u32[]{:S(2)}, u32[]{:S(2)}) collective-permute-start(bf16[128,768]{1,0:T(8,128)(2,1)S(1)} %get-tuple-element.25), channel_id=1, source_target_pairs={{0,64},{64,128},{128,192},{1,65},{65,129},{129,193},{2,66},{66,130... | collective-permute-start | bytes 589832 | tf_op jit(solution)/shard_map/ppermute | solution.py:21
where the time goes:
time: 279 us; the launch traced here: 278 us
  blocking collectives  204 us (73%)
  matrix products  28.3 us (10%)
  waiting for transfers between devices  22.1 us (8%)
  starting transfers between devices  16.5 us (6%)
  other arithmetic  3.25 us (1%)
  local copies, waits for them, and re-layouts  2.97 us (1%)
    all_to_all x5, blocking collectives, from_everyone(): return lax.all_to_all(copies, axis, split_axis=0, concat_axis=0, tiled=True)  94.1 us
    psum x10, blocking collectives, by_axis(): return functools.reduce(lax.psum, axes, array)  84.9 us
    all_to_all x3, blocking collectives, sent_and_summed(): lax.all_to_all(blocks, axis, split_axis=0, concat_axis=0, tiled=True)  24.6 us
    ppermute x5, waiting for transfers between devices, shifted(): return lax.ppermute(array, axis, pairs)  22.1 us
    dot_general x3, matrix products, primal_solve(): lax.dot_general(loads, schur_inverse, (((2,), (1,)), ((0,), (0,))), prefe...  15.3 us
    ppermute x5, starting transfers between devices, shifted(): return lax.ppermute(array, axis, pairs)  12.4 us
  transfers between devices with their start and end apart: 6, of which 5 were waited for; matrix products, arithmetic and copies ran while one was open for 2% of the time, Pallas kernels for 0%

commit v1 on v0

v1 whole, which is shorter than its diff:
```python
import functools

import jax
import jax.numpy as jnp
from jax import lax
from jax.experimental import pallas as pl
from jax.experimental.pallas import tpu as pltpu
from jax.sharding import Mesh
from jax.sharding import PartitionSpec as P

AXES = ("sub", "coarse_0", "coarse_1", "coarse_2", "coarse_3")
COARSE = AXES[1:]
LANES = 128
SOLVES = 3
F32 = jnp.float32
BF16 = jnp.bfloat16


def contract(a, b, da, db):
    return lax.dot_general(a, b, (((da,), (db,)), ((), ())), preferred_element_type=F32)


def mm(a, b):
    return contract(a, b, 1, 0)


def upper_lower(a):
    upper = a.astype(BF16)
    return upper, (a - upper.astype(F32)).astype(BF16)


def kernel(
    sizes,
    schur,
    coupling,
    coarse,
    cases,
    order,
    dofs,
    scene_loads,
    scene_weights,
    x_out,
    r_out,
    S,
    fwd,
    bwd,
    K,
    Kt,
    D,
    Dt,
    E,
    Et,
    entry,
    f,
    base,
    left,
    W,
    Wn,
    cv,
    T,
    R,
    G,
    V,
    face_send,
    face_recv,
    right_send,
    right_recv,
    prev_coupling,
    own_entry,
    prev_entry,
    dots,
    dots_a,
    dots_b,
    coef,
    load_sem,
    send_sem,
    recv_sem,
    last_send,
    last_recv,
):
    n_sub, nx, nh, ny, nk = sizes
    nz = nh * n_sub
    corners = dofs.shape[1]
    face = order.shape[1]
    column = n_sub * corners
    s, x, h, y, k = (lax.axis_index(a) for a in AXES)
    z = h * n_sub + s
    xy = x * ny + y
    group = ((x * nh + h) * ny + y) * nk + k

    def at(sub=None, cx=None, ch=None, cy=None, ck=None):
        return (
            s if sub is None else sub,
            x if cx is None else cx,
            h if ch is None else ch,
            y if cy is None else cy,
            k if ck is None else ck,
        )

    def z_at(dz, dk=0):
        other = lax.rem(z + dz, nz)
        return at(sub=lax.rem(other, n_sub), ch=other // n_sub, ck=lax.rem(k + dk, nk))

    def xy_at(dx, dy):
        return at(cx=lax.rem(x + dx, nx), cy=lax.rem(y + dy, ny))

    z_steps = [(dz, dk) for dk in range(nk) for dz in range(nz) if (dz, dk) != (0, 0)]
    xy_steps = [(dx, dy) for dx in range(nx) for dy in range(ny) if (dx, dy) != (0, 0)]
    xy_steps.sort(key=lambda d: -(min(d[0], nx - d[0]) + min(d[1], ny - d[1])))
    greeted = [z_at(*d) for d in z_steps] + [xy_at(*d) for d in xy_steps]

    barrier = pltpu.get_barrier_semaphore()
    for device in greeted:
        pl.semaphore_signal(barrier, inc=1, device_id=device, device_id_type=pl.DeviceIdType.MESH)
    loads = [pltpu.make_async_copy(schur.at[j], S.at[j], load_sem.at[j]) for j in range(2)]
    for load in loads:
        load.start()

    sent = []

    def remote(src, dst, send, recv, device):
        return pltpu.make_async_remote_copy(
            src_ref=src,
            dst_ref=dst,
            send_sem=send,
            recv_sem=recv,
            device_id=device,
            device_id_type=pl.DeviceIdType.MESH,
        )

    SEM_XY = nz
    SEM_K = SEM_XY + nx * ny
    SEM_E = SEM_K + nx
    SEM_FACE = SEM_E + n_sub
    SEM_RIGHT = SEM_FACE + 1
    SEM_INIT = SEM_RIGHT + 1

    def copy(slot, number, src, dst, device):
        return remote(src, dst, send_sem.at[slot, number], recv_sem.at[slot, number], device)

    def start(c):
        c.start()
        sent.append(c)
        return c

    def iota(shape, dim):
        return lax.broadcasted_iota(jnp.int32, shape, dim)

    lane = iota((scene_loads.shape[0], LANES), 1)
    mixing = jnp.where(lane == scene_loads[:, 0:1], scene_weights[:, 0:1], 0.0)
    mixing = mixing + jnp.where(lane == scene_loads[:, 1:2], scene_weights[:, 1:2], 0.0)
    mixing = mixing.T[: cases.shape[1]]
    mix_0, rest = upper_lower(mixing)
    rest = mixing - mix_0.astype(F32)
    mix_1, mix_2 = upper_lower(rest)
    mix = jnp.concatenate([mix_0, mix_1, mix_2], axis=0)
    for j in range(2):
        thrice = jnp.concatenate([cases[j]] * 3, axis=0)
        f[j] = contract(thrice, mix, 0, 0).astype(BF16)

    eye = (iota((corners, corners), 0) == iota((corners, corners), 1)).astype(BF16)
    entry[...] = jnp.zeros_like(entry)
    total = jnp.zeros((LANES, LANES), F32)
    stride = nx * nh * ny * nk * corners
    for j in range(2):
        shifted = dofs[j : j + 1, :] - group * corners
        local = shifted
        for a in range(1, n_sub):
            local = local - jnp.where(shifted >= a * stride, stride - corners, 0)
        table = (iota((LANES, corners), 0) == local).astype(F32).astype(BF16)
        rows = contract(eye, table, 1, 1)
        if j == 0:
            entry[corners : 2 * corners, :] = rows
            entry[2 * corners : 3 * corners, :] = rows
        else:
            entry[3 * corners : 4 * corners, :] = rows
            own_entry[...] = rows.astype(BF16)
        for part in upper_lower(mm(coupling[j], f[j])):
            total = total + mm(table, part)

    pl.semaphore_wait(barrier, len(greeted))

    def send_column(slot, total):
        for a in range(n_sub):
            T[slot, a] = total[a * corners : (a + 1) * corners].astype(BF16)
        copies = [
            start(copy(slot, dz, T.at[slot, lax.rem(z + dz, n_sub)], R.at[slot, z], z_at(dz)))
            for dz in range(1, nz)
        ]
        R[slot, z] = T[slot, s]
        return copies

    copies_b = send_column(0, total)

    coupling_copy = copy(
        0, SEM_INIT, coupling.at[1, :, face:], prev_coupling, at(sub=lax.rem(s + 1, n_sub))
    )
    entry_copy = copy(0, SEM_INIT + 1, own_entry, prev_entry, at(sub=lax.rem(s + 1, n_sub)))

    @pl.when(s < n_sub - 1)
    def _():
        entry_copy.start()
        coupling_copy.start()

    def build_permutations(j):
        row = order[j : j + 1, :]
        for b in range(0, face, LANES):
            ids = iota((LANES, face), 0) + b
            bwd[j, b : b + LANES, :] = (ids == row).astype(F32).astype(BF16)
        spread = jnp.broadcast_to(row.astype(F32), (LANES, face)).T
        for b in range(0, face, LANES):
            ids = (iota((face, LANES), 1) + b).astype(F32)
            fwd[j, :, b : b + LANES] = (spread == ids).astype(F32).astype(BF16)

    def build_coarse():
        wide = coarse[...].astype(F32)
        if column < LANES:
            wide = jnp.concatenate([wide, jnp.zeros((LANES - column, wide.shape[1]), F32)], axis=0)
        turned = wide.T
        for cx in range(nx):
            for ch in range(nh):
                for cy in range(ny):
                    for ck in range(nk):
                        src = (((cx * nh + ch) * ny + cy) * nk + ck) * corners
                        dst = (((ck * nx + cx) * ny + cy) * nh + ch) * corners
                        Kt[dst : dst + corners, :] = turned[src : src + corners, :]
        K[...] = Kt[...].T.astype(BF16)

    def build_corner(j, right):
        block = jnp.concatenate(
            [mm(right, bwd[j]), -coupling[j, :, :face].astype(F32)],
            axis=0,
        )
        above = 2 * corners * j
        below = LANES - above - 2 * corners
        parts = [block]
        if above:
            parts = [jnp.zeros((above, face), F32)] + parts
        if below:
            parts = parts + [jnp.zeros((below, face), F32)]
        block = jnp.concatenate(parts, axis=0)
        D[j] = block.astype(BF16)
        Dt[j] = block.T.astype(BF16)

    right_copies = [
        copy(i, SEM_RIGHT, right_send.at[i], right_recv.at[i], at(sub=lax.rem(s + 1, n_sub)))
        for i in range(SOLVES)
    ]
    face_copies = [
        copy(i, SEM_FACE, face_send.at[i], face_recv.at[i], at(sub=lax.rem(s + n_sub - 1, n_sub)))
        for i in range(SOLVES)
    ]

    def first_local(slot):
        right = mm(S[0, face:, :], f[0]).astype(BF16)
        left[0] = mm(S[0, :face, :], f[0])
        base[1] = mm(fwd[1], right)

    def second_local(slot):
        right_send[slot] = mm(S[1, face:, :], f[1]).astype(BF16)

        @pl.when(s < n_sub - 1)
        def _():
            right_copies[slot].start()

        base[1] = base[1] - mm(S[1, :face, :], f[1])

    def gather_start(slot, copies):
        for c in copies:
            c.wait_recv()
        halves = []
        for ch in range(nh):
            summed = R[slot, ch * n_sub].astype(F32)
            for a in range(1, n_sub):
                summed = summed + R[slot, ch * n_sub + a].astype(F32)
            halves.append(summed)
        G[slot, k * nx * ny + xy] = jnp.concatenate(halves, axis=0).astype(BF16)
        piece = G.at[slot, k * nx * ny + xy]
        return {
            d: start(copy(slot, SEM_XY + d[0] * ny + d[1], piece, piece, xy_at(*d)))
            for d in xy_steps
        }

    def gather_end(slot, copies):
        passed = []
        for dx in sorted(range(nx), key=lambda d: min(d, nx - d)):
            for dy in range(ny):
                if (dx, dy) in copies:
                    copies[dx, dy].wait_recv()
            first = k * nx * ny + lax.rem(x - dx + nx, nx) * ny
            block = G.at[slot, pl.ds(first, ny)]
            passed.append(
                start(copy(slot, SEM_K + dx, block, block, at(ck=lax.rem(k + 1, nk))))
            )
        for c in passed:
            c.wait_recv()
        gathered = G[slot]
        gathered = gathered.reshape(gathered.shape[0] * gathered.shape[1], LANES)
        V[slot, s] = mm(K[...], gathered)[:column].astype(BF16)
        piece = V.at[slot, s]
        return [
            start(copy(slot, SEM_E + ds, piece, piece, at(sub=lax.rem(s + ds, n_sub))))
            for ds in range(1, n_sub)
        ]

    def base_of_first(slot):
        @pl.when(s > 0)
        def _():
            right_copies[slot].wait_recv()
            base[0] = mm(fwd[0], right_recv[slot]) - left[0]

        @pl.when(s == 0)
        def _():
            base[0] = jnp.zeros_like(left[0])

    def image(slot, copies):
        for c in copies:
            c.wait_recv()
        summed = V[slot, 0].astype(F32)
        for a in range(1, n_sub):
            summed = summed + V[slot, a].astype(F32)
        cv[0:column, :] = summed.astype(BF16)
        picked = mm(E[...], cv[...]).astype(BF16)
        for j in range(2):
            W[slot, j] = base[j] + mm(Dt[j], picked)

    def turn(slot):
        for j in range(2):
            Wn[slot, j] = W[slot, j].T

    build_permutations(1)
    for load in loads:
        load.wait()
    second = mm(S[1, face:, :], f[1]).astype(BF16)
    right_send[0] = second

    @pl.when(s < n_sub - 1)
    def _():
        right_copies[0].start()

    copies_c = gather_start(0, copies_b)
    first_local(0)
    base[1] = base[1] - mm(S[1, :face, :], f[1])
    build_coarse()
    cv[...] = jnp.zeros_like(cv)
    copies_e = gather_end(0, copies_c)
    build_permutations(0)
    build_corner(1, coupling[0, :, face:])

    @pl.when(s > 0)
    def _():
        coupling_copy.wait_recv()
        entry_copy.wait_recv()
        build_corner(0, prev_coupling[...])
        entry[0:corners, :] = prev_entry[...].astype(F32)

    @pl.when(s == 0)
    def _():
        D[0] = jnp.zeros_like(D[0])
        Dt[0] = jnp.zeros_like(Dt[0])

    E[...] = entry[...].astype(BF16)
    turned = entry[...].T.astype(BF16)
    Et[:, 0:LANES] = turned
    Et[:, LANES:] = turned
    base_of_first(0)
    image(0, copies_e)

    def product(a, b):
        summed = jnp.sum(a[0] * b[0], axis=0, keepdims=True)
        return summed + jnp.sum(a[1] * b[1], axis=0, keepdims=True)

    for slot in range(1, SOLVES):
        v = [W[slot - 1, j].astype(BF16) for j in range(2)]
        terms = mm(D[0], v[0]) + mm(D[1], v[1])
        copies_b = send_column(slot, mm(Et[...], jnp.concatenate(upper_lower(terms), axis=0)))
        face_send[slot] = mm(bwd[0], v[0]).astype(BF16)

        @pl.when(s > 0)
        def _():
            face_copies[slot].start()

        f[0, face:, :] = mm(bwd[1], v[1]).astype(BF16)
        for j in range(2):
            f[j, :face, :] = -v[j]
        first_local(slot)
        copies_c = gather_start(slot, copies_b)

        @pl.when(s < n_sub - 1)
        def _():
            face_copies[slot].wait_recv()
            f[1, face:, :] = face_recv[slot]

        @pl.when(s == n_sub - 1)
        def _():
            f[1, face:, :] = jnp.zeros((face, LANES), BF16)

        second_local(slot)
        copies_e = gather_end(slot, copies_c)
        turn(slot - 1)
        if slot == 1:
            dots[...] = jnp.zeros_like(dots)
            dots[0:1, :] = product(W[0], W[0])
        else:
            dots[1:2, :] = product(W[0], W[1])
            dots[2:3, :] = product(W[1], W[1])
        base_of_first(slot)
        image(slot, copies_e)

    dots[3:4, :] = product(W[0], W[2])
    dots[4:5, :] = product(W[1], W[2])

    here = z * nk + k
    copies = [
        start(
            remote(
                dots,
                dots_a.at[here],
                last_send.at[i],
                last_recv.at[i],
                z_at(*d),
            )
        )
        for i, d in enumerate(z_steps)
    ]
    dots_a[here] = dots[...]
    turn(SOLVES - 1)
    for c in copies:
        c.wait_recv()
    dots_b[xy] = jnp.sum(dots_a[...], axis=0)
    copies = [
        start(
            remote(
                dots_b.at[xy],
                dots_b.at[xy],
                last_send.at[len(z_steps) + i],
                last_recv.at[len(z_steps) + i],
                xy_at(*d),
            )
        )
        for i, d in enumerate(xy_steps)
    ]
    for c in copies:
        c.wait_recv()
    sums = jnp.sum(dots_b[...], axis=0)
    rr, rw, ww, rv, wv = (sums[i : i + 1, :] for i in range(5))
    step = rr / rw
    left_over = rr - 2.0 * step * rw + step * step * ww
    gain = 1.0 + left_over / rr
    curvature = gain * gain * rw - gain * step * (rv + ww) + step * step * wv
    second_step = left_over / curvature
    coef[...] = jnp.zeros_like(coef)
    coef[0:1, :] = step + second_step * gain
    coef[1:2, :] = second_step * step
    columns = coef[...].T
    c_one, c_two = columns[:, 0:1], columns[:, 1:2]
    for j in range(2):
        x_out[j] = c_one * Wn[0, j] - c_two * Wn[1, j]
        r_out[j] = Wn[0, j] - c_one * Wn[1, j] + c_two * Wn[2, j]

    for c in sent:
        c.wait_send()

    @pl.when(s < n_sub - 1)
    def _():
        entry_copy.wait_send()
        coupling_copy.wait_send()
        for c in right_copies:
            c.wait_send()

    @pl.when(s > 0)
    def _():
        for c in face_copies[1:]:
            c.wait_send()


def per_device(sizes, schur, coupling, coarse, cases, order, dofs, scene_loads, scene_weights):
    n_sub, nx, nh, ny, nk = sizes
    nz, nxy = nh * n_sub, nx * ny
    corners, face, scenes = dofs.shape[1], order.shape[1], scene_weights.shape[0]
    column = n_sub * corners
    coarse = coarse.reshape(column, coarse.shape[3])
    gathered = coarse.shape[1]
    sems = nz + nxy + nx + n_sub + 4
    last = nz * nk + nxy - 2
    vmem = pl.BlockSpec(memory_space=pltpu.VMEM)
    out = jax.ShapeDtypeStruct((2, scenes, face), F32)
    return pl.pallas_call(
        functools.partial(kernel, sizes),
        out_shape=(out, out),
        in_specs=[pl.BlockSpec(memory_space=pl.ANY)] + [vmem] * 7,
        out_specs=(vmem, vmem),
        scratch_shapes=[
            pltpu.VMEM(schur.shape, BF16),
            pltpu.VMEM((2, face, face), BF16),
            pltpu.VMEM((2, face, face), BF16),
            pltpu.VMEM((LANES, gathered), BF16),
            pltpu.VMEM((gathered, LANES), F32),
            pltpu.VMEM((2, LANES, face), BF16),
            pltpu.VMEM((2, face, LANES), BF16),
            pltpu.VMEM((LANES, LANES), BF16),
            pltpu.VMEM((LANES, 2 * LANES), BF16),
            pltpu.VMEM((LANES, LANES), F32),
            pltpu.VMEM((2, 2 * face, LANES), BF16),
            pltpu.VMEM((2, face, LANES), F32),
            pltpu.VMEM((1, face, LANES), F32),
            pltpu.VMEM((SOLVES, 2, face, LANES), F32),
            pltpu.VMEM((SOLVES, 2, LANES, face), F32),
            pltpu.VMEM((LANES, LANES), BF16),
            pltpu.VMEM((SOLVES, n_sub, corners, LANES), BF16),
            pltpu.VMEM((SOLVES, nz, corners, LANES), BF16),
            pltpu.VMEM((SOLVES, nk * nxy, nh * corners, LANES), BF16),
            pltpu.VMEM((SOLVES, n_sub, column, LANES), BF16),
            pltpu.VMEM((SOLVES, face, LANES), BF16),
            pltpu.VMEM((SOLVES, face, LANES), BF16),
            pltpu.VMEM((SOLVES, face, LANES), BF16),
            pltpu.VMEM((SOLVES, face, LANES), BF16),
            pltpu.VMEM((corners, face), BF16),
            pltpu.VMEM((corners, LANES), BF16),
            pltpu.VMEM((corners, LANES), BF16),
            pltpu.VMEM((8, LANES), F32),
            pltpu.VMEM((nz * nk, 8, LANES), F32),
            pltpu.VMEM((nxy, 8, LANES), F32),
            pltpu.VMEM((LANES, LANES), F32),
            pltpu.SemaphoreType.DMA((2,)),
            pltpu.SemaphoreType.DMA((SOLVES, sems)),
            pltpu.SemaphoreType.DMA((SOLVES, sems)),
            pltpu.SemaphoreType.DMA((last,)),
            pltpu.SemaphoreType.DMA((last,)),
        ],
        compiler_params=pltpu.CompilerParams(collective_id=0, has_side_effects=True),
    )(schur, coupling, coarse, cases, order, dofs, scene_loads, scene_weights)


def solution(mesh):
    if mesh.devices.size == 256:
        sizes = (mesh.shape["sub"], 4, 2, 4, 2)
    else:
        sizes = (mesh.shape["sub"], mesh.shape["coarse"] // 4, 2, 1, 2)
    finer = Mesh(mesh.devices.reshape(sizes), AXES)
    return jax.shard_map(
        functools.partial(per_device, sizes),
        mesh=finer,
        in_specs=(
            P(AXES, None, None),
            P(AXES, None, None),
            P(None, COARSE, None, "sub"),
            P(AXES, None, None),
            P(AXES, None),
            P(AXES, None),
            P(),
            P(),
        ),
        out_specs=(P(AXES, None, None), P(AXES, None, None)),
        check_vma=False,
    )
```

time: 279 us -> 80.6 us (0.29)
  blocking collectives: 204 us -> 0 us
  Pallas kernels: 0 us -> 72.8 us
  matrix products: 28.3 us -> 0 us
  waiting for transfers between devices: 22.1 us -> 0 us
  starting transfers between devices: 16.5 us -> 0 us
  local copies, waits for them, and re-layouts: 2.97 us -> 6.95 us
  other arithmetic: 3.25 us -> 0 us
    all_to_all x8 -> x0, blocking collectives: 119 us -> none  [the longest x5 94.1 us: from_everyone(): return lax.all_to_all(copies, axis, split_axis=0, concat_axis=0, tiled=True)]
    psum x10 -> x0, blocking collectives: 84.9 us -> none  [by_axis(): return functools.reduce(lax.psum, axes, array)]
    pallas_call x0 -> x1, Pallas kernels: none -> 72.8 us  [per_device(): pl.pallas_call(functools.partial(kernel, sizes), out_shape=(out, out), in...]
    dot_general x24 -> x0, matrix products: 28.3 us -> none  [the longest x3 15.3 us: primal_solve(): lax.dot_general(loads, schur_inverse, (((2,), (1,)), ((0,), (0,))), prefe...]
    ppermute x5 -> x0, waiting for transfers between devices: 22.1 us -> none  [shifted(): return lax.ppermute(array, axis, pairs)]
    ppermute x5 -> x0, starting transfers between devices: 12.4 us -> none  [shifted(): return lax.ppermute(array, axis, pairs)]
    unnamed x12 -> x4, local copies, waits for them, and re-layouts: 1.85 us -> 6.95 us
    all_to_all x1 -> x0, starting transfers between devices: 4.12 us -> none  [from_everyone(): return lax.all_to_all(copies, axis, split_axis=0, concat_axis=0, tiled=True)]
  transfers between devices with their start and end apart: 6 -> 0, of which waited for: 5 -> 0; matrix products, arithmetic and copies ran while one was open for 2% -> 0% of each run, Pallas kernels for 0% -> 0%
where the time goes in v1:
time: 80.6 us; the launch traced here: 80.4 us
  Pallas kernels  72.8 us (90%)
  local copies, waits for them, and re-layouts  6.95 us (9%)
    pallas_call x1, Pallas kernels, per_device(): pl.pallas_call(functools.partial(kernel, sizes), out_shape=(out, out), in...  72.8 us
    unnamed x4, local copies, waits for them, and re-layouts  6.95 us

profile of v1, /device:TPU:1, one launch (start us, length us, event | category | flops | bytes accessed | tf_op | source)
XLA Modules:
  0.0 80.4 jit_solution(17085965057908047460)
XLA Ops:
  0.6 1.4 %copy.10.scene_loads = s32[128,2]{1,0:T(8,128)} copy(s32[128,2]{0,1:T(2,128)} %param.14) | data formatting | bytes 2048 | tf_op args[6]
  2.0 1.4 %copy.11.scene_weights = f32[128,2]{1,0:T(8,128)} copy(f32[128,2]{0,1:T(2,128)} %param.15) | data formatting | bytes 2048 | tf_op args[7]
  3.5 72.8 %shard_map.95 = (f32[2,128,768]{2,1,0:T(8,128)}, f32[2,128,768]{2,1,0:T(8,128)}) custom-call(bf16[2,1536,1536]{2,1,0:T(8,128)(2,1)} %schur.1, bf16[2,24,1536]{2,1,0:T(8,128)(2,1)} %coupling.1, bf16[96,1536]{1,0:T(8,128)(2,1)} %bitcast.1, bf16[2,16,1536]{2,1,0:T(8,128)(2,1)} %cases.1, s32[2,768]{1,0:T(2,128)} %order.1, s32[2,24]{1,0:T(2,128)} %dofs.1, ...), custom_call_target="tpu_custom_call" | custom-call | tf_op jit(solution)/shard_map/pallas_call | solution.py:488
  76.3 2.1 %copy.14 = f32[2,128,768]{2,1,0:T(8,128)} copy(f32[2,128,768]{2,1,0:T(8,128)} %get-tuple-element.4) | data formatting | bytes 1572864
  78.3 2.1 %copy.15 = f32[2,128,768]{2,1,0:T(8,128)} copy(f32[2,128,768]{2,1,0:T(8,128)} %get-tuple-element.5) | data formatting | bytes 1572864

commit v2 on v1

v2 whole, which is shorter than its diff:
```python
import functools

import jax
import jax.numpy as jnp
from jax import lax
from jax.experimental import pallas as pl
from jax.experimental.pallas import tpu as pltpu
from jax.sharding import Mesh
from jax.sharding import PartitionSpec as P

AXES = ("sub", "coarse_0", "coarse_1", "coarse_2", "coarse_3")
COARSE = AXES[1:]
LANES = 128
SOLVES = 3
VMEM_BYTES = 44 << 20
F32 = jnp.float32
BF16 = jnp.bfloat16


def contract(a, b, da, db):
    return lax.dot_general(a, b, (((da,), (db,)), ((), ())), preferred_element_type=F32)


def mm(a, b):
    return contract(a, b, 1, 0)


def upper_lower(a):
    upper = a.astype(BF16)
    return upper, (a - upper.astype(F32)).astype(BF16)


def kernel(
    sizes,
    schur,
    coupling_in,
    coarse_in,
    cases_in,
    order_in,
    dofs_in,
    scene_loads_in,
    scene_weights_in,
    w_0,
    w_1,
    w_2,
    coef_out,
    S,
    coupling,
    coarse,
    cases,
    order,
    dofs,
    scene_loads,
    scene_weights,
    fwd,
    bwd,
    K,
    Kt,
    Y,
    Yt,
    Z,
    E,
    Et,
    entry,
    f,
    w,
    base,
    Tb,
    H,
    H2,
    cv,
    T,
    R,
    G,
    V,
    A,
    left_send,
    left_recv,
    right_send,
    right_recv,
    own_order,
    own_entry,
    prev_coupling,
    prev_entry,
    next_coupling,
    next_entry,
    next_order,
    dots,
    dots_a,
    dots_b,
    coef,
    W,
    load_sem,
    send_sem,
    recv_sem,
    once_send,
    once_recv,
    last_send,
    last_recv,
):
    n_sub, nx, nh, ny, nk = sizes
    nz = nh * n_sub
    corners = dofs.shape[1]
    face = order.shape[1]
    column = n_sub * corners
    s, x, h, y, k = (lax.axis_index(a) for a in AXES)
    z = h * n_sub + s
    xy = x * ny + y
    group = ((x * nh + h) * ny + y) * nk + k
    has_next = s < n_sub - 1
    has_prev = s > 0

    def at(sub=None, cx=None, ch=None, cy=None, ck=None):
        return (
            s if sub is None else sub,
            x if cx is None else cx,
            h if ch is None else ch,
            y if cy is None else cy,
            k if ck is None else ck,
        )

    def z_at(dz, dk=0):
        other = lax.rem(z + dz, nz)
        return at(sub=lax.rem(other, n_sub), ch=other // n_sub, ck=lax.rem(k + dk, nk))

    def xy_at(dx, dy):
        return at(cx=lax.rem(x + dx, nx), cy=lax.rem(y + dy, ny))

    def sub_at(ds):
        return at(sub=lax.rem(s + ds, n_sub))

    after, before = sub_at(1), sub_at(n_sub - 1)
    z_steps = [(dz, dk) for dk in range(nk) for dz in range(nz) if (dz, dk) != (0, 0)]
    xy_steps = [(dx, dy) for dx in range(nx) for dy in range(ny) if (dx, dy) != (0, 0)]
    xy_steps.sort(key=lambda d: -(min(d[0], nx - d[0]) + min(d[1], ny - d[1])))
    greeted = [z_at(*d) for d in z_steps] + [xy_at(*d) for d in xy_steps]

    barrier = pltpu.get_barrier_semaphore()
    for device in greeted:
        pl.semaphore_signal(barrier, inc=1, device_id=device, device_id_type=pl.DeviceIdType.MESH)
    loads = [
        pltpu.make_async_copy(src, dst, load_sem.at[i])
        for i, (src, dst) in enumerate(
            (
                (scene_loads_in, scene_loads),
                (scene_weights_in, scene_weights),
                (dofs_in, dofs),
                (cases_in, cases),
                (coupling_in, coupling),
                (order_in, order),
                (schur.at[1], S.at[1]),
                (schur.at[0], S.at[0]),
                (coarse_in, coarse),
            )
        )
    ]
    for load in loads:
        load.start()
    early, load_order, load_second, load_first, load_coarse = loads[:5], *loads[5:]

    sent = []

    def remote(src, dst, send, recv, device):
        return pltpu.make_async_remote_copy(
            src_ref=src,
            dst_ref=dst,
            send_sem=send,
            recv_sem=recv,
            device_id=device,
            device_id_type=pl.DeviceIdType.MESH,
        )

    SEM_XY = nz
    SEM_K = SEM_XY + nx * ny
    SEM_E = SEM_K + nx
    SEM_LEFT = SEM_E + n_sub
    SEM_RIGHT = SEM_LEFT + 1

    def copy(slot, number, src, dst, device):
        return remote(src, dst, send_sem.at[slot, number], recv_sem.at[slot, number], device)

    def once(number, src, dst, device):
        return remote(src, dst, once_send.at[number], once_recv.at[number], device)

    def start(c):
        c.start()
        sent.append(c)
        return c

    def iota(shape, dim):
        return lax.broadcasted_iota(jnp.int32, shape, dim)

    def stacked(blocks, width):
        rows = sum(b.shape[0] for b in blocks)
        rest = [jnp.zeros((LANES - rows, width), F32)] if rows < LANES else []
        return jnp.concatenate([b.astype(F32) for b in blocks] + rest, axis=0)

    for load in early:
        load.wait()
    case = iota((cases.shape[1], LANES), 0)
    mixing = jnp.where(case == scene_loads[0:1, :], scene_weights[0:1, :], 0.0)
    mixing = mixing + jnp.where(case == scene_loads[1:2, :], scene_weights[1:2, :], 0.0)
    mix_0 = mixing.astype(BF16)
    mix_1, mix_2 = upper_lower(mixing - mix_0.astype(F32))
    mix = jnp.concatenate([mix_0, mix_1, mix_2], axis=0)
    for j in range(2):
        thrice = jnp.concatenate([cases[j]] * 3, axis=0)
        f[j] = contract(thrice, mix, 0, 0).astype(BF16)

    eye = (iota((corners, corners), 0) == iota((corners, corners), 1)).astype(BF16)
    entry[...] = jnp.zeros_like(entry)
    total = jnp.zeros((LANES, LANES), F32)
    stride = nx * nh * ny * nk * corners
    for j in range(2):
        shifted = dofs[j : j + 1, :] - group * corners
        local = shifted
        for a in range(1, n_sub):
            local = local - jnp.where(shifted >= a * stride, stride - corners, 0)
        table = (iota((LANES, corners), 0) == local).astype(F32).astype(BF16)
        rows = contract(eye, table, 1, 1)
        entry[(j + 1) * corners : (j + 2) * corners, :] = rows
        own_entry[j] = rows.astype(BF16)
        for part in upper_lower(mm(coupling[j], f[j])):
            total = total + mm(table, part)
    load_order.wait()
    row_a = order[0:1, :].astype(F32)
    own_order[...] = jnp.broadcast_to(row_a, own_order.shape)

    @pl.when(jnp.logical_not(has_prev))
    def _():
        prev_coupling[...] = jnp.zeros_like(prev_coupling)
        prev_entry[...] = jnp.zeros_like(prev_entry)

    @pl.when(jnp.logical_not(has_next))
    def _():
        next_coupling[...] = jnp.zeros_like(next_coupling)
        next_entry[...] = jnp.zeros_like(next_entry)
        next_order[...] = jnp.zeros_like(next_order)

    pl.semaphore_wait(barrier, len(greeted))

    def send_column(slot, total):
        for a in range(n_sub):
            T[slot, a] = total[a * corners : (a + 1) * corners].astype(BF16)
        copies = [
            start(copy(slot, dz, T.at[slot, lax.rem(z + dz, n_sub)], R.at[slot, z], z_at(dz)))
            for dz in range(1, nz)
        ]
        R[slot, z] = T[slot, s]
        return copies

    copies_b = send_column(0, total)

    to_next = [
        once(0, own_entry.at[1], prev_entry, after),
        once(1, coupling.at[1, :, face:], prev_coupling, after),
    ]
    to_prev = [
        once(2, own_entry.at[0], next_entry, before),
        once(3, own_order, next_order, before),
        once(4, coupling.at[0, :, :face], next_coupling, before),
    ]
    to_next += [
        copy(i, SEM_RIGHT, right_send.at[i], right_recv.at[i], after) for i in range(SOLVES)
    ]
    to_prev += [
        copy(i, SEM_LEFT, left_send.at[i], left_recv.at[i], before) for i in range(SOLVES)
    ]
    init_next, rights = to_next[:2], to_next[2:]
    init_prev, lefts = to_prev[:3], to_prev[3:]

    @pl.when(has_next)
    def _():
        for c in init_next:
            c.start()

    @pl.when(has_prev)
    def _():
        for c in init_prev:
            c.start()

    def build_permutations(j, row):
        for b in range(0, face, LANES):
            ids = (iota((LANES, face), 0) + b).astype(F32)
            bwd[j, b : b + LANES, :] = (ids == row).astype(F32).astype(BF16)
        spread = jnp.broadcast_to(row, (LANES, face)).T
        for b in range(0, face, LANES):
            ids = (iota((face, LANES), 1) + b).astype(F32)
            fwd[j, :, b : b + LANES] = (spread == ids).astype(F32).astype(BF16)

    def build_coarse():
        turned = stacked([coarse[...]], coarse.shape[1]).T
        for cx in range(nx):
            for ch in range(nh):
                for cy in range(ny):
                    for ck in range(nk):
                        src = (((cx * nh + ch) * ny + cy) * nk + ck) * corners
                        dst = (((ck * nx + cx) * ny + cy) * nh + ch) * corners
                        Kt[dst : dst + corners, :] = turned[src : src + corners, :]
        K[...] = Kt[...].T.astype(BF16)

    def local_products(slot):
        right = mm(S[1, face:, :], f[1])
        right_send[slot] = right.astype(BF16)

        @pl.when(has_next)
        def _():
            rights[slot].start()

        if slot == 0:
            load_first.wait()
        left = mm(S[0, :face, :], f[0])
        left_send[slot] = left.astype(BF16)

        @pl.when(has_prev)
        def _():
            lefts[slot].start()

        return left, right

    def local_rest(slot, left, right):
        inner = mm(S[0, face:, :], f[0])
        inner_left = mm(S[1, :face, :], f[1])
        w[0, :face, :] = left.astype(BF16)
        w[0, face:, :] = inner.astype(BF16)
        w[1, :face, :] = inner_left.astype(BF16)
        w[1, face:, :] = right.astype(BF16)
        base[1] = mm(fwd[1], w[0, face:, :]) - inner_left
        base[2] = mm(fwd[2], w[1, face:, :])
        return inner, inner_left

    def column_base():
        terms = mm(Z[0], w[0]) + mm(Z[1], w[1])
        Tb[...] = mm(Et[...], jnp.concatenate(upper_lower(terms), axis=0))

    def gather_start(slot, copies):
        for c in copies:
            c.wait_recv()
        halves = []
        for ch in range(nh):
            summed = R[slot, ch * n_sub].astype(F32)
            for a in range(1, n_sub):
                summed = summed + R[slot, ch * n_sub + a].astype(F32)
            halves.append(summed)
        G[slot, k * nx * ny + xy] = jnp.concatenate(halves, axis=0).astype(BF16)
        piece = G.at[slot, k * nx * ny + xy]
        started = {
            d: start(copy(slot, SEM_XY + d[0] * ny + d[1], piece, piece, xy_at(*d)))
            for d in xy_steps
        }
        if slot < SOLVES - 1:
            return started, []
        own = halves[0]
        for ch in range(1, nh):
            own = jnp.where(h == ch, halves[ch], own)
        A[s] = own.astype(BF16)
        piece = A.at[s]
        return started, [
            start(once(ONCE_A + ds, piece, piece, sub_at(ds))) for ds in range(1, n_sub)
        ]

    ONCE_H = 4
    ONCE_A = ONCE_H + n_sub - 1

    def gather_end(slot, copies):
        passed = []
        for dx in sorted(range(nx), key=lambda d: min(d, nx - d)):
            for dy in range(ny):
                if (dx, dy) in copies:
                    copies[dx, dy].wait_recv()
            first = k * nx * ny + lax.rem(x - dx + nx, nx) * ny
            block = G.at[slot, pl.ds(first, ny)]
            passed.append(
                start(copy(slot, SEM_K + dx, block, block, at(ck=lax.rem(k + 1, nk))))
            )
        for c in passed:
            c.wait_recv()
        gathered = G[slot]
        gathered = gathered.reshape(gathered.shape[0] * gathered.shape[1], LANES)
        return mm(K[...], gathered)

    def share(slot, part):
        V[slot, s] = part[:column].astype(BF16)
        piece = V.at[slot, s]
        return [start(copy(slot, SEM_E + ds, piece, piece, sub_at(ds))) for ds in range(1, n_sub)]

    def outer_bases(slot):
        @pl.when(has_prev)
        def _():
            rights[slot].wait_recv()
            base[0] = mm(fwd[0], right_recv[slot]) - left_send[slot].astype(F32)

        @pl.when(jnp.logical_not(has_prev))
        def _():
            base[0] = jnp.zeros((face, LANES), F32)

        @pl.when(has_next)
        def _():
            lefts[slot].wait_recv()
            base[2] = base[2] - left_recv[slot].astype(F32)

        @pl.when(jnp.logical_not(has_next))
        def _():
            base[2] = jnp.zeros((face, LANES), F32)

    def image(slot, copies):
        for c in copies:
            c.wait_recv()
        summed = V[slot, 0].astype(F32)
        for a in range(1, n_sub):
            summed = summed + V[slot, a].astype(F32)
        cv[0:column, :] = summed.astype(BF16)
        picked = mm(E[...], cv[...]).astype(BF16)
        out = []
        for j in range(2 if slot == SOLVES - 1 else 3):
            whole = base[j] + mm(Yt[j], picked)
            if j < 2:
                W[slot, j] = whole
            out.append(whole.astype(BF16))
        return out

    def turn(slot):
        for j in range(2):
            (w_0, w_1, w_2)[slot][j] = W[slot, j].T

    def product(a, b):
        summed = jnp.sum(a[0].astype(F32) * b[0], axis=0, keepdims=True)
        return summed + jnp.sum(a[1].astype(F32) * b[1], axis=0, keepdims=True)

    load_second.wait()
    left, right = local_products(0)
    build_permutations(1, order[1:2, :].astype(F32))
    copies_c, _ = gather_start(0, copies_b)

    build_permutations(0, row_a)

    @pl.when(has_prev)
    def _():
        for c in init_next:
            c.wait_recv()

    entry[0:corners, :] = prev_entry[...].astype(F32)
    none = jnp.zeros((corners, face), F32)
    keep_prev = jnp.where(has_prev, 1.0, 0.0).astype(F32)
    keep_next = jnp.where(has_next, 1.0, 0.0).astype(F32)
    left_a = coupling[0, :, :face].astype(F32) * keep_prev
    right_a = coupling[0, :, face:]
    left_b = coupling[1, :, :face]
    right_b = coupling[1, :, face:].astype(F32) * keep_next
    moved_a = mm(prev_coupling[...], bwd[0])
    moved_b = mm(right_a, bwd[1])
    blocks_a = stacked([moved_a, -left_a], face)
    blocks_b = stacked([none, moved_b, -left_b.astype(F32)], face)
    for j, blocks in ((0, blocks_a), (1, blocks_b)):
        Y[j] = blocks.astype(BF16)
        Yt[j] = blocks.T.astype(BF16)

    @pl.when(has_next)
    def _():
        for c in init_prev:
            c.wait_recv()

    entry[3 * corners : 4 * corners, :] = next_entry[...].astype(F32)
    E[...] = entry[...].astype(BF16)
    turned = entry[...].T.astype(BF16)
    Et[:, 0:LANES] = turned
    Et[:, LANES:] = turned

    square = contract(Y[0], Y[0], 1, 1) + contract(Y[1], Y[1], 1, 1)
    upper, lower = upper_lower(square)
    square = mm(upper, E[...]) + mm(lower, E[...])
    square = mm(Et[...], jnp.concatenate(upper_lower(square), axis=0))
    H[s] = square[:column]
    piece = H.at[s]
    copies_h = [start(once(ONCE_H + ds, piece, piece, sub_at(ds))) for ds in range(1, n_sub)]

    build_permutations(2, next_order[0:1, :])
    local_rest(0, left, right)
    moved_c = mm(right_b.astype(BF16), bwd[2])
    blocks_c = stacked([none, none, moved_c, -next_coupling[...].astype(F32)], face)
    Yt[2] = blocks_c.T.astype(BF16)
    Z[0, :, :face] = stacked([-moved_a, left_a], face).astype(BF16)
    Z[0, :, face:] = stacked([none, right_a, -mm(left_b, fwd[1])], face).astype(BF16)
    Z[1, :, :face] = stacked([none, -moved_b, left_b], face).astype(BF16)
    Z[1, :, face:] = stacked([none, none, right_b, -mm(next_coupling[...], fwd[2])], face).astype(
        BF16
    )
    column_base()
    load_coarse.wait()
    build_coarse()
    cv[...] = jnp.zeros_like(cv)
    dots[...] = jnp.zeros_like(dots)
    for c in copies_h:
        c.wait_recv()
    square = H[0]
    for a in range(1, n_sub):
        square = square + H[a]
    H2[:, 0:LANES], H2[:, LANES:] = upper_lower(square)

    def send_next(slot, part):
        rounded = part.astype(BF16)
        change = mm(H2[...], jnp.concatenate([rounded, rounded], axis=0))
        return send_column(slot, Tb[0:column, :] + change)

    part = gather_end(0, copies_c)
    copies_b = send_next(1, part)
    copies_e = share(0, part)
    outer_bases(0)

    for slot in range(1, SOLVES):
        v = image(slot - 1, copies_e)
        f[0, :face, :] = -v[0]
        f[0, face:, :] = mm(bwd[1], v[1]).astype(BF16)
        f[1, :face, :] = -v[1]
        f[1, face:, :] = mm(bwd[2], v[2]).astype(BF16)
        copies_c, copies_a = gather_start(slot, copies_b)
        left, right = local_products(slot)
        inner, inner_left = local_rest(slot, left, right)
        if slot < SOLVES - 1:
            column_base()
        else:
            local = jnp.sum(f[0, :face, :].astype(F32) * left, axis=0, keepdims=True)
            local = local + jnp.sum(f[0, face:, :].astype(F32) * inner, axis=0, keepdims=True)
            local = local + jnp.sum(f[1, :face, :].astype(F32) * inner_left, axis=0, keepdims=True)
            local = local + jnp.sum(f[1, face:, :].astype(F32) * right, axis=0, keepdims=True)
            dots[1:2, :] = product(W[0], W[1])
            dots[2:3, :] = product(W[1], W[1])
            for c in copies_a:
                c.wait_recv()
        turn(slot - 1)
        if slot == 1:
            dots[0:1, :] = product(W[0], W[0])
        part = gather_end(slot, copies_c)
        if slot < SOLVES - 1:
            copies_b = send_next(slot + 1, part)
        else:
            for a in range(n_sub):
                block = part[a * corners : (a + 1) * corners]
                local = local + jnp.sum(A[a].astype(F32) * block, axis=0, keepdims=True)
            dots[3:4, :] = local
            here = z * nk + k
            copies = [
                start(remote(dots, dots_a.at[here], last_send.at[i], last_recv.at[i], z_at(*d)))
                for i, d in enumerate(z_steps)
            ]
            dots_a[here] = dots[...]
        copies_e = share(slot, part)
        if slot < SOLVES - 1:
            outer_bases(slot)

    for c in copies:
        c.wait_recv()
    dots_b[xy] = jnp.sum(dots_a[...], axis=0)
    more = len(z_steps)
    copies = [
        start(
            remote(
                dots_b.at[xy],
                dots_b.at[xy],
                last_send.at[more + i],
                last_recv.at[more + i],
                xy_at(*d),
            )
        )
        for i, d in enumerate(xy_steps)
    ]
    outer_bases(SOLVES - 1)
    image(SOLVES - 1, copies_e)
    turn(SOLVES - 1)
    for c in copies:
        c.wait_recv()
    sums = jnp.sum(dots_b[...], axis=0)
    rr, rw, ww, wv = (sums[i : i + 1, :] for i in range(4))
    step = rr / rw
    left_over = rr - 2.0 * step * rw + step * step * ww
    gain = 1.0 + left_over / rr
    curvature = gain * gain * rw - 2.0 * gain * step * ww + step * step * wv
    second_step = left_over / curvature
    coef[...] = jnp.zeros_like(coef)
    coef[0:1, :] = step + second_step * gain
    coef[1:2, :] = second_step * step
    coef_out[...] = coef[...].T

    for c in sent:
        c.wait_send()

    @pl.when(has_next)
    def _():
        for c in to_next:
            c.wait_send()

    @pl.when(has_prev)
    def _():
        for c in to_prev:
            c.wait_send()


def per_device(sizes, schur, coupling, coarse, cases, order, dofs, scene_loads, scene_weights):
    n_sub, nx, nh, ny, nk = sizes
    nz, nxy = nh * n_sub, nx * ny
    corners, face, scenes = dofs.shape[1], order.shape[1], scene_weights.shape[0]
    column = n_sub * corners
    coarse = coarse.reshape(column, coarse.shape[3])
    gathered = coarse.shape[1]
    sems = nz + nxy + nx + n_sub + 4
    last = nz * nk + nxy - 2
    vmem = pl.BlockSpec(memory_space=pltpu.VMEM)
    out = jax.ShapeDtypeStruct((2, scenes, face), F32)
    operands = (schur, coupling, coarse, cases, order, dofs, scene_loads.T, scene_weights.T)
    operands = [pltpu.with_memory_space_constraint(a, pltpu.HBM) for a in operands]
    w_0, w_1, w_2, coef = pl.pallas_call(
        functools.partial(kernel, sizes),
        out_shape=(out, out, out, jax.ShapeDtypeStruct((LANES, LANES), F32)),
        in_specs=[pl.BlockSpec(memory_space=pltpu.HBM)] * 8,
        out_specs=(vmem,) * 4,
        scratch_shapes=[
            pltpu.VMEM(schur.shape, BF16),
            pltpu.VMEM(coupling.shape, BF16),
            pltpu.VMEM(coarse.shape, BF16),
            pltpu.VMEM(cases.shape, BF16),
            pltpu.VMEM(order.shape, jnp.int32),
            pltpu.VMEM(dofs.shape, jnp.int32),
            pltpu.VMEM((2, scenes), jnp.int32),
            pltpu.VMEM((2, scenes), F32),
            pltpu.VMEM((3, face, face), BF16),
            pltpu.VMEM((3, face, face), BF16),
            pltpu.VMEM((LANES, gathered), BF16),
            pltpu.VMEM((gathered, LANES), F32),
            pltpu.VMEM((2, LANES, face), BF16),
            pltpu.VMEM((3, face, LANES), BF16),
            pltpu.VMEM((2, LANES, 2 * face), BF16),
            pltpu.VMEM((LANES, LANES), BF16),
            pltpu.VMEM((LANES, 2 * LANES), BF16),
            pltpu.VMEM((LANES, LANES), F32),
            pltpu.VMEM((2, 2 * face, LANES), BF16),
            pltpu.VMEM((2, 2 * face, LANES), BF16),
            pltpu.VMEM((3, face, LANES), F32),
            pltpu.VMEM((LANES, LANES), F32),
            pltpu.VMEM((n_sub, column, LANES), F32),
            pltpu.VMEM((column, 2 * LANES), BF16),
            pltpu.VMEM((LANES, LANES), BF16),
            pltpu.VMEM((SOLVES, n_sub, corners, LANES), BF16),
            pltpu.VMEM((SOLVES, nz, corners, LANES), BF16),
            pltpu.VMEM((SOLVES, nk * nxy, nh * corners, LANES), BF16),
            pltpu.VMEM((SOLVES, n_sub, column, LANES), BF16),
            pltpu.VMEM((n_sub, corners, LANES), BF16),
            pltpu.VMEM((SOLVES, face, LANES), BF16),
            pltpu.VMEM((SOLVES, face, LANES), BF16),
            pltpu.VMEM((SOLVES, face, LANES), BF16),
            pltpu.VMEM((SOLVES, face, LANES), BF16),
            pltpu.VMEM((8, face), F32),
            pltpu.VMEM((2, corners, LANES), BF16),
            pltpu.VMEM((corners, face), BF16),
            pltpu.VMEM((corners, LANES), BF16),
            pltpu.VMEM((corners, face), BF16),
            pltpu.VMEM((corners, LANES), BF16),
            pltpu.VMEM((8, face), F32),
            pltpu.VMEM((8, LANES), F32),
            pltpu.VMEM((nz * nk, 8, LANES), F32),
            pltpu.VMEM((nxy, 8, LANES), F32),
            pltpu.VMEM((LANES, LANES), F32),
            pltpu.VMEM((SOLVES, 2, face, LANES), F32),
            pltpu.SemaphoreType.DMA((9,)),
            pltpu.SemaphoreType.DMA((SOLVES, sems)),
            pltpu.SemaphoreType.DMA((SOLVES, sems)),
            pltpu.SemaphoreType.DMA((5 + 2 * n_sub,)),
            pltpu.SemaphoreType.DMA((5 + 2 * n_sub,)),
            pltpu.SemaphoreType.DMA((last,)),
            pltpu.SemaphoreType.DMA((last,)),
        ],
        compiler_params=pltpu.CompilerParams(
            collective_id=0, has_side_effects=True, vmem_limit_bytes=VMEM_BYTES
        ),
    )(*operands)
    c_one, c_two = coef[:, 0:1], coef[:, 1:2]
    return c_one * w_0 - c_two * w_1, w_0 - c_one * w_1 + c_two * w_2


def solution(mesh):
    if mesh.devices.size == 256:
        sizes = (mesh.shape["sub"], 4, 2, 4, 2)
    else:
        sizes = (mesh.shape["sub"], mesh.shape["coarse"] // 4, 2, 1, 2)
    finer = Mesh(mesh.devices.reshape(sizes), AXES)
    return jax.shard_map(
        functools.partial(per_device, sizes),
        mesh=finer,
        in_specs=(
            P(AXES, None, None),
            P(AXES, None, None),
            P(None, COARSE, None, "sub"),
            P(AXES, None, None),
            P(AXES, None),
            P(AXES, None),
            P(),
            P(),
        ),
        out_specs=(P(AXES, None, None), P(AXES, None, None)),
        check_vma=False,
    )
```

time: 80.6 us -> 64.8 us (0.80)
  Pallas kernels: 72.8 us -> 62.5 us
  local copies, waits for them, and re-layouts: 6.95 us -> 0.17 us
  other arithmetic: 0 us -> 1.43 us
    pallas_call x1, Pallas kernels: 72.8 us -> 62.5 us  [per_device(): pl.pallas_call(functools.partial(kernel, sizes), out_shape=(out, out, out...]
    unnamed x4 -> x0, local copies, waits for them, and re-layouts: 6.95 us -> none
    add x0 -> x1, other arithmetic: none -> 1.43 us  [per_device(): return (c_one * w_0 - c_two * w_1, w_0 - c_one * w_1 + c_two * w_2)]
where the time goes in v2:
time: 64.8 us; the launch traced here: 64.7 us
  Pallas kernels  62.5 us (96%)
  other arithmetic  1.43 us (2%)
    pallas_call x1, Pallas kernels, per_device(): pl.pallas_call(functools.partial(kernel, sizes), out_shape=(out, out, out...  62.5 us
    add x1, other arithmetic, per_device(): return (c_one * w_0 - c_two * w_1, w_0 - c_one * w_1 + c_two * w_2)  1.43 us

profile of v2, /device:TPU:1, one launch (start us, length us, event | category | flops | bytes accessed | tf_op | source)
XLA Modules:
  0.0 64.7 jit_solution(3548118596279483129)
XLA Ops:
  0.6 62.5 %shard_map.95 = (f32[2,128,768]{2,1,0:T(8,128)S(1)}, f32[2,128,768]{2,1,0:T(8,128)S(1)}, f32[2,128,768]{2,1,0:T(8,128)S(1)}, f32[128,128]{1,0:T(8,128)S(1)}) custom-call(bf16[2,1536,1536]{2,1,0:T(8,128)(2,1)} %schur.1, bf16[2,24,1536]{2,1,0:T(8,128)(2,1)} %coupling_in.1, bf16[96,1536]{1,0:T(8,128)(2,1)} %bitcast.3, bf16[2,16,1536]{2,1,0:T(8,128)(2,1)} %cases_in.1, ...), custom_call_target="tpu_custom_call" | custom-call | tf_op jit(solution)/shard_map/pallas_call | solution.py:611
  63.1 0.2 slice_reduce_fusion.1
  63.3 1.4 %multiply_add_fusion = (f32[2,128,768]{2,1,0:T(8,128)}, f32[2,128,768]{2,1,0:T(8,128)}) fusion(f32[2,128,768]{2,1,0:T(8,128)S(1)} %get-tuple-element.9, f32[2,128,768]{2,1,0:T(8,128)S(1)} %get-tuple-element.7, f32[2,128,768]{2,1,0:T(8,128)S(1)} %get-tuple-element.8, f32[128]{0:T(128)S(1)} %get-tuple-element.11, f32[128]{0:T(128)S(1)} %get-tuple-element.10), kind=kLoop, calls=%fused_computation | loop fusion | flops 1376256 | bytes 3933184 | tf_op jit(solution)/shard_map/add | solution.py:676

commit v3 on v2

--- a/solution.py
+++ b/solution.py
@@ -90,6 +90,8 @@
     dots_b,
     coef,
     W,
+    wb,
+    SC,
     load_sem,
     send_sem,
     recv_sem,
@@ -299,35 +301,42 @@
                         Kt[dst : dst + corners, :] = turned[src : src + corners, :]
         K[...] = Kt[...].T.astype(BF16)
 
-    def local_products(slot):
-        right = mm(S[1, face:, :], f[1])
-        right_send[slot] = right.astype(BF16)
+    lower_half, upper_half = slice(0, face), slice(face, 2 * face)
+    RIGHT, LEFT, INNER, INNER_LEFT = (
+        (1, upper_half),
+        (0, lower_half),
+        (0, upper_half),
+        (1, lower_half),
+    )
+
+    def direct(part):
+        return mm(S[part], f[part[0]])
+
+    def send_outer(slot, right, left):
+        right_send[slot] = right().astype(BF16)
 
         @pl.when(has_next)
         def _():
             rights[slot].start()
 
-        if slot == 0:
-            load_first.wait()
-        left = mm(S[0, :face, :], f[0])
-        left_send[slot] = left.astype(BF16)
+        left_send[slot] = left().astype(BF16)
 
         @pl.when(has_prev)
         def _():
             lefts[slot].start()
 
-        return left, right
-
-    def local_rest(slot, left, right):
-        inner = mm(S[0, face:, :], f[0])
-        inner_left = mm(S[1, :face, :], f[1])
-        w[0, :face, :] = left.astype(BF16)
-        w[0, face:, :] = inner.astype(BF16)
-        w[1, :face, :] = inner_left.astype(BF16)
-        w[1, face:, :] = right.astype(BF16)
-        base[1] = mm(fwd[1], w[0, face:, :]) - inner_left
-        base[2] = mm(fwd[2], w[1, face:, :])
-        return inner, inner_left
+        w[RIGHT] = right_send[slot]
+        w[LEFT] = left_send[slot]
+
+    def fill(v):
+        f[0, :face, :] = -v[0]
+        f[0, face:, :] = mm(bwd[1], v[1]).astype(BF16)
+        f[1, :face, :] = -v[1]
+        f[1, face:, :] = mm(bwd[2], v[2]).astype(BF16)
+
+    def coarse_response(j):
+        for half in (lower_half, upper_half):
+            SC[j, half, 0:LANES], SC[j, half, LANES:] = upper_lower(direct((j, half)))
 
     def column_base():
         terms = mm(Z[0], w[0]) + mm(Z[1], w[1])
@@ -362,7 +371,7 @@
     ONCE_H = 4
     ONCE_A = ONCE_H + n_sub - 1
 
-    def gather_end(slot, copies):
+    def gather_pass(slot, copies):
         passed = []
         for dx in sorted(range(nx), key=lambda d: min(d, nx - d)):
             for dy in range(ny):
@@ -373,6 +382,9 @@
             passed.append(
                 start(copy(slot, SEM_K + dx, block, block, at(ck=lax.rem(k + 1, nk))))
             )
+        return passed
+
+    def gather_end(slot, passed):
         for c in passed:
             c.wait_recv()
         gathered = G[slot]
@@ -384,7 +396,9 @@
         piece = V.at[slot, s]
         return [start(copy(slot, SEM_E + ds, piece, piece, sub_at(ds))) for ds in range(1, n_sub)]
 
-    def outer_bases(slot):
+    def bases(slot):
+        base[1] = mm(fwd[1], w[0, face:, :]) - w[1, :face, :].astype(F32)
+
         @pl.when(has_prev)
         def _():
             rights[slot].wait_recv()
@@ -397,27 +411,24 @@
         @pl.when(has_next)
         def _():
             lefts[slot].wait_recv()
-            base[2] = base[2] - left_recv[slot].astype(F32)
+            base[2] = mm(fwd[2], w[1, face:, :]) - left_recv[slot].astype(F32)
 
         @pl.when(jnp.logical_not(has_next))
         def _():
             base[2] = jnp.zeros((face, LANES), F32)
 
-    def image(slot, copies):
+    def picked_values(slot, copies):
         for c in copies:
             c.wait_recv()
         summed = V[slot, 0].astype(F32)
         for a in range(1, n_sub):
             summed = summed + V[slot, a].astype(F32)
         cv[0:column, :] = summed.astype(BF16)
-        picked = mm(E[...], cv[...]).astype(BF16)
-        out = []
-        for j in range(2 if slot == SOLVES - 1 else 3):
-            whole = base[j] + mm(Yt[j], picked)
-            if j < 2:
-                W[slot, j] = whole
-            out.append(whole.astype(BF16))
-        return out
+        return mm(E[...], cv[...]).astype(BF16)
+
+    def image(slot, picked):
+        for j in range(2):
+            W[slot, j] = base[j] + mm(Yt[j], picked)
 
     def turn(slot):
         for j in range(2):
@@ -428,11 +439,21 @@
         return summed + jnp.sum(a[1].astype(F32) * b[1], axis=0, keepdims=True)
 
     load_second.wait()
-    left, right = local_products(0)
+
+    def second_then_first():
+        load_first.wait()
+        return direct(LEFT)
+
+    send_outer(0, lambda: direct(RIGHT), second_then_first)
+    w[INNER] = direct(INNER).astype(BF16)
+    w[INNER_LEFT] = direct(INNER_LEFT).astype(BF16)
     build_permutations(1, order[1:2, :].astype(F32))
+    build_permutations(0, row_a)
+    load_coarse.wait()
+    build_coarse()
+    cv[...] = jnp.zeros_like(cv)
+    dots[...] = jnp.zeros_like(dots)
     copies_c, _ = gather_start(0, copies_b)
-
-    build_permutations(0, row_a)
 
     @pl.when(has_prev)
     def _():
@@ -475,7 +496,6 @@
     copies_h = [start(once(ONCE_H + ds, piece, piece, sub_at(ds))) for ds in range(1, n_sub)]
 
     build_permutations(2, next_order[0:1, :])
-    local_rest(0, left, right)
     moved_c = mm(right_b.astype(BF16), bwd[2])
     blocks_c = stacked([none, none, moved_c, -next_coupling[...].astype(F32)], face)
     Yt[2] = blocks_c.T.astype(BF16)
@@ -485,11 +505,11 @@
     Z[1, :, face:] = stacked([none, none, right_b, -mm(next_coupling[...], fwd[2])], face).astype(
         BF16
     )
+    fill((Yt[0], Yt[1], Yt[2]))
+    coarse_response(1)
+    passed = gather_pass(0, copies_c)
     column_base()
-    load_coarse.wait()
-    build_coarse()
-    cv[...] = jnp.zeros_like(cv)
-    dots[...] = jnp.zeros_like(dots)
+    coarse_response(0)
     for c in copies_h:
         c.wait_recv()
     square = H[0]
@@ -502,35 +522,45 @@
         change = mm(H2[...], jnp.concatenate([rounded, rounded], axis=0))
         return send_column(slot, Tb[0:column, :] + change)
 
-    part = gather_end(0, copies_c)
+    part = gather_end(0, passed)
     copies_b = send_next(1, part)
     copies_e = share(0, part)
-    outer_bases(0)
+    bases(0)
 
     for slot in range(1, SOLVES):
-        v = image(slot - 1, copies_e)
-        f[0, :face, :] = -v[0]
-        f[0, face:, :] = mm(bwd[1], v[1]).astype(BF16)
-        f[1, :face, :] = -v[1]
-        f[1, face:, :] = mm(bwd[2], v[2]).astype(BF16)
+        fill([base[j].astype(BF16) for j in range(3)])
+        for part in (RIGHT, LEFT, INNER):
+            wb[part] = direct(part)
         copies_c, copies_a = gather_start(slot, copies_b)
-        left, right = local_products(slot)
-        inner, inner_left = local_rest(slot, left, right)
+        wb[INNER_LEFT] = direct(INNER_LEFT)
+        picked = picked_values(slot - 1, copies_e)
+        twice = jnp.concatenate([picked, picked], axis=0)
+
+        def whole(part):
+            return wb[part] + mm(SC[part], twice)
+
+        send_outer(slot, lambda: whole(RIGHT), lambda: whole(LEFT))
+        w[INNER] = whole(INNER).astype(BF16)
+        w[INNER_LEFT] = whole(INNER_LEFT).astype(BF16)
+        image(slot - 1, picked)
         if slot < SOLVES - 1:
+            passed = gather_pass(slot, copies_c)
             column_base()
+            turn(slot - 1)
+            dots[0:1, :] = product(W[0], W[0])
         else:
-            local = jnp.sum(f[0, :face, :].astype(F32) * left, axis=0, keepdims=True)
-            local = local + jnp.sum(f[0, face:, :].astype(F32) * inner, axis=0, keepdims=True)
-            local = local + jnp.sum(f[1, :face, :].astype(F32) * inner_left, axis=0, keepdims=True)
-            local = local + jnp.sum(f[1, face:, :].astype(F32) * right, axis=0, keepdims=True)
+            last = base[2] + mm(Yt[2], picked)
+            fill([W[slot - 1, 0].astype(BF16), W[slot - 1, 1].astype(BF16), last.astype(BF16)])
+            passed = gather_pass(slot, copies_c)
+            local = jnp.zeros((1, LANES), F32)
+            for j in range(2):
+                terms = f[j].astype(F32) * w[j].astype(F32)
+                local = local + jnp.sum(terms, axis=0, keepdims=True)
             dots[1:2, :] = product(W[0], W[1])
             dots[2:3, :] = product(W[1], W[1])
             for c in copies_a:
                 c.wait_recv()
-        turn(slot - 1)
-        if slot == 1:
-            dots[0:1, :] = product(W[0], W[0])
-        part = gather_end(slot, copies_c)
+        part = gather_end(slot, passed)
         if slot < SOLVES - 1:
             copies_b = send_next(slot + 1, part)
         else:
@@ -545,8 +575,9 @@
             ]
             dots_a[here] = dots[...]
         copies_e = share(slot, part)
-        if slot < SOLVES - 1:
-            outer_bases(slot)
+        if slot == SOLVES - 1:
+            turn(slot - 1)
+        bases(slot)
 
     for c in copies:
         c.wait_recv()
@@ -564,8 +595,7 @@
         )
         for i, d in enumerate(xy_steps)
     ]
-    outer_bases(SOLVES - 1)
-    image(SOLVES - 1, copies_e)
+    image(SOLVES - 1, picked_values(SOLVES - 1, copies_e))
     turn(SOLVES - 1)
     for c in copies:
         c.wait_recv()
@@ -660,6 +690,8 @@
             pltpu.VMEM((nxy, 8, LANES), F32),
             pltpu.VMEM((LANES, LANES), F32),
             pltpu.VMEM((SOLVES, 2, face, LANES), F32),
+            pltpu.VMEM((2, 2 * face, LANES), F32),
+            pltpu.VMEM((2, 2 * face, 2 * LANES), BF16),
             pltpu.SemaphoreType.DMA((9,)),
             pltpu.SemaphoreType.DMA((SOLVES, sems)),
             pltpu.SemaphoreType.DMA((SOLVES, sems)),

time: 64.8 us -> 61.7 us (0.952)
  Pallas kernels: 62.5 us -> 59.1 us
    pallas_call x1, Pallas kernels: 62.5 us -> 59.1 us  [per_device(): pl.pallas_call(functools.partial(kernel, sizes), out_shape=(out, out, out...]
where the time goes in v3:
time: 61.7 us; the launch traced here: 61.4 us
  Pallas kernels  59.1 us (96%)
  other arithmetic  1.43 us (2%)
  between operations  0.64 us (1%)
    pallas_call x1, Pallas kernels, per_device(): pl.pallas_call(functools.partial(kernel, sizes), out_shape=(out, out, out...  59.1 us
    add x1, other arithmetic, per_device(): return (c_one * w_0 - c_two * w_1, w_0 - c_one * w_1 + c_two * w_2)  1.43 us

profile of v3, /device:TPU:1, one launch (start us, length us, event | category | flops | bytes accessed | tf_op | source)
XLA Modules:
  0.0 61.4 jit_solution(11072229952456239054)
XLA Ops:
  0.6 59.1 %shard_map.95 = (f32[2,128,768]{2,1,0:T(8,128)S(1)}, f32[2,128,768]{2,1,0:T(8,128)S(1)}, f32[2,128,768]{2,1,0:T(8,128)S(1)}, f32[128,128]{1,0:T(8,128)S(1)}) custom-call(bf16[2,1536,1536]{2,1,0:T(8,128)(2,1)} %schur.1, bf16[2,24,1536]{2,1,0:T(8,128)(2,1)} %coupling_in.1, bf16[96,1536]{1,0:T(8,128)(2,1)} %bitcast.3, bf16[2,16,1536]{2,1,0:T(8,128)(2,1)} %cases_in.1, ...), custom_call_target="tpu_custom_call" | custom-call | tf_op jit(solution)/shard_map/pallas_call | solution.py:641
  59.7 0.2 slice_reduce_fusion.1
  59.9 1.4 %multiply_add_fusion = (f32[2,128,768]{2,1,0:T(8,128)}, f32[2,128,768]{2,1,0:T(8,128)}) fusion(f32[2,128,768]{2,1,0:T(8,128)S(1)} %get-tuple-element.9, f32[2,128,768]{2,1,0:T(8,128)S(1)} %get-tuple-element.7, f32[2,128,768]{2,1,0:T(8,128)S(1)} %get-tuple-element.8, f32[128]{0:T(128)S(1)} %get-tuple-element.11, f32[128]{0:T(128)S(1)} %get-tuple-element.10), kind=kLoop, calls=%fused_computation | loop fusion | flops 1376256 | bytes 3933184 | tf_op jit(solution)/shard_map/add | solution.py:708

commit v4 on v3

--- a/solution.py
+++ b/solution.py
@@ -43,7 +43,8 @@
     w_0,
     w_1,
     w_2,
-    coef_out,
+    one_out,
+    two_out,
     S,
     coupling,
     coarse,
@@ -137,9 +138,6 @@
     xy_steps.sort(key=lambda d: -(min(d[0], nx - d[0]) + min(d[1], ny - d[1])))
     greeted = [z_at(*d) for d in z_steps] + [xy_at(*d) for d in xy_steps]
 
-    barrier = pltpu.get_barrier_semaphore()
-    for device in greeted:
-        pl.semaphore_signal(barrier, inc=1, device_id=device, device_id_type=pl.DeviceIdType.MESH)
     loads = [
         pltpu.make_async_copy(src, dst, load_sem.at[i])
         for i, (src, dst) in enumerate(
@@ -158,6 +156,9 @@
     ]
     for load in loads:
         load.start()
+    barrier = pltpu.get_barrier_semaphore()
+    for device in greeted:
+        pl.semaphore_signal(barrier, inc=1, device_id=device, device_id_type=pl.DeviceIdType.MESH)
     early, load_order, load_second, load_first, load_coarse = loads[:5], *loads[5:]
 
     sent = []
@@ -385,11 +386,16 @@
         return passed
 
     def gather_end(slot, passed):
+        def half(core):
+            rows = G[slot, pl.ds(core * nx * ny, nx * ny)]
+            wide = rows.shape[0] * rows.shape[1]
+            part = K[:, pl.ds(pl.multiple_of(core * wide, wide), wide)]
+            return mm(part, rows.reshape(wide, LANES))
+
+        own = half(k)
         for c in passed:
             c.wait_recv()
-        gathered = G[slot]
-        gathered = gathered.reshape(gathered.shape[0] * gathered.shape[1], LANES)
-        return mm(K[...], gathered)
+        return own + half(1 - k)
 
     def share(slot, part):
         V[slot, s] = part[:column].astype(BF16)
@@ -529,10 +535,11 @@
 
     for slot in range(1, SOLVES):
         fill([base[j].astype(BF16) for j in range(3)])
-        for part in (RIGHT, LEFT, INNER):
+        for part in (RIGHT, LEFT):
             wb[part] = direct(part)
         copies_c, copies_a = gather_start(slot, copies_b)
-        wb[INNER_LEFT] = direct(INNER_LEFT)
+        for part in (INNER, INNER_LEFT):
+            wb[part] = direct(part)
         picked = picked_values(slot - 1, copies_e)
         twice = jnp.concatenate([picked, picked], axis=0)
 
@@ -609,7 +616,9 @@
     coef[...] = jnp.zeros_like(coef)
     coef[0:1, :] = step + second_step * gain
     coef[1:2, :] = second_step * step
-    coef_out[...] = coef[...].T
+    columns = coef[...].T
+    one_out[...] = jnp.broadcast_to(columns[:, 0:1], one_out.shape)
+    two_out[...] = jnp.broadcast_to(columns[:, 1:2], two_out.shape)
 
     for c in sent:
         c.wait_send()
@@ -638,11 +647,11 @@
     out = jax.ShapeDtypeStruct((2, scenes, face), F32)
     operands = (schur, coupling, coarse, cases, order, dofs, scene_loads.T, scene_weights.T)
     operands = [pltpu.with_memory_space_constraint(a, pltpu.HBM) for a in operands]
-    w_0, w_1, w_2, coef = pl.pallas_call(
+    w_0, w_1, w_2, one, two = pl.pallas_call(
         functools.partial(kernel, sizes),
-        out_shape=(out, out, out, jax.ShapeDtypeStruct((LANES, LANES), F32)),
+        out_shape=(out, out, out) + (jax.ShapeDtypeStruct((scenes, face), F32),) * 2,
         in_specs=[pl.BlockSpec(memory_space=pltpu.HBM)] * 8,
-        out_specs=(vmem,) * 4,
+        out_specs=(vmem,) * 5,
         scratch_shapes=[
             pltpu.VMEM(schur.shape, BF16),
             pltpu.VMEM(coupling.shape, BF16),
@@ -704,8 +713,7 @@
             collective_id=0, has_side_effects=True, vmem_limit_bytes=VMEM_BYTES
         ),
     )(*operands)
-    c_one, c_two = coef[:, 0:1], coef[:, 1:2]
-    return c_one * w_0 - c_two * w_1, w_0 - c_one * w_1 + c_two * w_2
+    return one * w_0 - two * w_1, w_0 - one * w_1 + two * w_2
 
 
 def solution(mesh):

time: 61.7 us -> 60.6 us (0.982)
  no operation moved by 1% of the time
where the time goes in v4:
time: 60.6 us; the launch traced here: 60.5 us
  Pallas kernels  58.5 us (97%)
  other arithmetic  1.34 us (2%)
  between operations  0.64 us (1%)
    pallas_call x1, Pallas kernels, per_device(): pl.pallas_call(functools.partial(kernel, sizes), out_shape=(out, out, out...  58.5 us
    add x1, other arithmetic, per_device(): return (one * w_0 - two * w_1, w_0 - one * w_1 + two * w_2)  1.34 us

profile of v4, /device:TPU:1, one launch (start us, length us, event | category | flops | bytes accessed | tf_op | source)
XLA Modules:
  0.0 60.5 jit_solution(10178369850431529868)
XLA Ops:
  0.6 58.5 %shard_map.95 = (f32[2,128,768]{2,1,0:T(8,128)S(1)}, f32[2,128,768]{2,1,0:T(8,128)S(1)}, f32[2,128,768]{2,1,0:T(8,128)S(1)}, f32[128,768]{1,0:T(8,128)S(1)}, f32[128,768]{1,0:T(8,128)S(1)}) custom-call(bf16[2,1536,1536]{2,1,0:T(8,128)(2,1)} %schur.1, bf16[2,24,1536]{2,1,0:T(8,128)(2,1)} %coupling_in.1, bf16[96,1536]{1,0:T(8,128)(2,1)} %bitcast.3, ...), custom_call_target="tpu_custom_call" | custom-call | tf_op jit(solution)/shard_map/pallas_call | solution.py:650
  59.2 1.3 %multiply_add_fusion = (f32[2,128,768]{2,1,0:T(8,128)}, f32[2,128,768]{2,1,0:T(8,128)}) fusion(f32[2,128,768]{2,1,0:T(8,128)S(1)} %get-tuple-element.11, f32[2,128,768]{2,1,0:T(8,128)S(1)} %get-tuple-element.8, f32[2,128,768]{2,1,0:T(8,128)S(1)} %get-tuple-element.10, f32[128,768]{1,0:T(8,128)S(1)} %get-tuple-element.9, f32[128,768]{1,0:T(8,128)S(1)} %get-tuple-element.7), kind=kLoop, calls=%fused_computation | loop fusion | flops 1376256 | bytes 4718592 | tf_op jit(solution)/shard_map/add | solution.py:716
